TPU v7x, 32 devices: a whole 2x2x4 slice. The times are simulated.
32 devices in a mesh: seq: 16 (over z, y, x), mem: 2 (over core).
Axes of the slice: x: 2, y: 2, z: 4, core: 2. Of those that a mesh axis runs over, the one named last changes fastest.
Arguments:
- tokens: bfloat16 [16384, 768], P(('seq', 'mem')), may hold values from -6 to 6
- memory: bfloat16 [4096, 768], P(('seq', 'mem')), may hold values from -6 to 6
- lengths: int32 [16], P('seq'), may hold values from 256 to 1024, as said below
- tokens_cotangent: bfloat16 [16384, 768], P(('seq', 'mem')), may hold values from -6 to 6
- memory_cotangent: bfloat16 [4096, 768], P(('seq', 'mem')), may hold values from -6 to 6
- projections: float32 [6, 768, 768], P(None, ('seq', 'mem')), may hold values from -1 to 1
- output_maps: float32 [2, 768, 768], P(None, ('seq', 'mem')), may hold values from -1 to 1
- expand_weight: float32 [768, 3072], P(('seq', 'mem')), may hold values from -0.21875 to 0.21875
- shrink_weight: float32 [3072, 768], P(('seq', 'mem')), may hold values from -0.109375 to 0.109375
- projection_bias: float32 [6, 768], P(None, ('seq', 'mem')), may hold values from -2 to 2
- norm_gain: float32 [3, 768], P(None, ('seq', 'mem')), may hold values from 0.5 to 1.5
- norm_bias: float32 [3, 768], P(None, ('seq', 'mem')), may hold values from -2 to 2
- expand_bias: float32 [3072], P(('seq', 'mem')), may hold values from -2 to 2
- shrink_bias: float32 [768], P(('seq', 'mem')), may hold values from -2 to 2
Outputs:
- new_tokens: float32 [16384, 768], P(('seq', 'mem'))
- new_memory: float32 [4096, 768], P(('seq', 'mem'))
- tokens_grad: float32 [16384, 768], P(('seq', 'mem'))
- memory_grad: float32 [4096, 768], P(('seq', 'mem'))
- projections_grad: float32 [6, 768, 768], P(None, ('seq', 'mem'))
- output_maps_grad: float32 [2, 768, 768], P(None, ('seq', 'mem'))
- expand_weight_grad: float32 [768, 3072], P(('seq', 'mem'))
- shrink_weight_grad: float32 [3072, 768], P(('seq', 'mem'))
- projection_bias_grad: float32 [6, 768], P(None, ('seq', 'mem'))
- norm_gain_grad: float32 [3, 768], P(None, ('seq', 'mem'))
- norm_bias_grad: float32 [3, 768], P(None, ('seq', 'mem'))
- expand_bias_grad: float32 [3072], P(('seq', 'mem'))
- shrink_bias_grad: float32 [768], P(('seq', 'mem'))
Inputs may be any that keep to these rules, and one draw needn't show every extreme that they name: `lengths`: every sequence has at least a quarter of its 1024 slots live; some sequence fills all 1024 in every draw; live tokens come first.
All inputs are finite; a program needn't handle non-finite values.
Results may differ from a plain program's by a relative error of at most 0.015.
Values may be sent and summed in bfloat16 or wider, within the bound.
A program may use at most 256 MiB of HBM per device.

v0:
```python
import functools

import jax
import jax.numpy as jnp
from jax import lax
from jax.experimental import pallas as pl
from jax.experimental.pallas import tpu as pltpu
from jax.sharding import PartitionSpec as P

HEAD = 64
epsilon = 1e-05
MESH = pl.DeviceIdType.MESH
LOW = jnp.bfloat16
F32 = jnp.float32
AXES = ("seq", "mem")


def matmul(left, right):
    return jnp.dot(left, right, preferred_element_type=F32)


def matmul_left(left, right):
    return lax.dot_general(left, right, (((0,), (0,)), ((), ())), preferred_element_type=F32)


def matmul_right(left, right):
    return lax.dot_general(left, right, (((1,), (1,)), ((), ())), preferred_element_type=F32)


def to_low(values):
    return values.astype(LOW)


def column_sum(values):
    return jnp.sum(values.astype(F32), axis=0)


def swap(values):
    return lax.ppermute(values, "mem", [(0, 1), (1, 0)])


def join(own, other, axis=0):
    first = lax.axis_index("mem") == 0
    return jnp.where(
        first, jnp.concatenate([own, other], axis), jnp.concatenate([other, own], axis)
    )


def both(values, axis=0):
    return join(values, swap(values), axis)


def half(values, index, axis):
    size = values.shape[axis] // 2
    return lax.dynamic_slice_in_dim(values, index * size, size, axis)


FORWARD = (
    (0, 0), (15, 0), (16, 0), (0, 1), (15, 1), (1, 0), (16, 1), (0, 2), (0, 3), (2, 0), (1, 1), (3, 0), (2, 1),
    (1, 2), "q", (3, 1), (4, 0), (2, 2), "k", (5, 0), (3, 2), "v", "pf0", (4, 1), (6, 0), "pf1", (5, 1), "pf2", "cx",
    (7, 0), (4, 2), (6, 1), (4, 3), "yp", (5, 2), (8, 0), "ln0", (7, 1), (9, 0), (6, 2), "ku", (8, 1), (10, 0),
    (7, 2), "qu", "uf0", (9, 1), (11, 0), "uf1", "uf2", (8, 2), (10, 1), (12, 0), "ux", (8, 3), (9, 2), "att",
    (9, 3), (11, 1), (13, 0), (10, 2), (12, 1), (14, 0), (10, 3), "w0", "w2", (11, 2), (13, 1), (11, 3), (12, 2),
    (14, 1), (12, 3), "w1", "w3", (13, 2), (14, 2), (13, 3), (14, 3), (15, 2), (15, 3), (16, 2), (16, 3), "nar",
)
BACKWARD = (
    (0, 0), (1, 0), "dha", "dhb", (2, 0), (3, 0), "de0", (0, 1), (1, 1), "de1", (0, 2), (1, 2), "dm0", (2, 1),
    (3, 1), "dm1", (2, 2), (3, 2), (4, 0), (5, 0), "mix", (1, 3), (0, 3), "gm1", "ua0", (2, 3), (3, 3), "ua1",
    (6, 0), (7, 0), (4, 1), (5, 1), "ua2", (1, 4), "pk", (4, 2), (5, 2), "g3", (0, 4), "g45", (6, 1), (7, 1), "gm0",
    (2, 4), (6, 2), (7, 2), "pa0", (8, 0), (5, 3), (4, 3), (9, 0), "pa1", (3, 4), "pa2", (6, 3), (7, 3), (10, 0),
    (11, 0), "g0", (8, 1), (9, 1), (5, 4), "g12", (8, 2), (9, 2), (16, 0), "tok0", (4, 4), (16, 1), "out0", (10, 1),
    (11, 1), "out1", "fin", (6, 4), (10, 2), (11, 2), (12, 0), (9, 3), (8, 3), (13, 0), (7, 4), (16, 2), (11, 3),
    (10, 3), (9, 4), (14, 0), (12, 1), (13, 1), (12, 2), (8, 4), (15, 0), (16, 3), (13, 2), (14, 1), (12, 3),
    (11, 4), (14, 2), (15, 1), (10, 4), (13, 3), (15, 2), (15, 3), (14, 3), (16, 4), (12, 4), (13, 4), (15, 4),
    (14, 4),
)


def place(seq):
    return lax.div(seq, 4), lax.rem(lax.div(seq, 2), 2), lax.rem(seq, 2)


def peers(seq, core, far_count):
    far, row, column = place(seq)
    flat = lambda f, r, c: f * 4 + r * 2 + c
    far_peers = [lax.rem(far + k, far_count) for k in range(1, far_count)]
    return {
        "far": [(flat(f, row, column), core) for f in far_peers],
        "far_index": far_peers,
        "column": (flat(far, row, 1 - column), core),
        "row": (flat(far, 1 - row, column), core),
        "core": (seq, 1 - core),
    }


def greet(targets):
    barrier = pltpu.get_barrier_semaphore()
    for target in targets:
        pl.semaphore_signal(barrier, inc=1, device_id=target, device_id_type=MESH)
    pl.semaphore_wait(barrier, len(targets))


class Gather:
    def __init__(self, where, to, first, own, at, shared, sems):
        self.where, self.to, self.own, self.at, self.shared = where, to, own, at, shared
        self.first, self.second = first, ("row" if first == "column" else "column")
        self.send, self.recv = sems
        self.started = []

    def _column(self, near):
        far, row, column = self.where
        row, column = (
            (1 - row if "row" in near else row),
            (1 - column if "column" in near else column),
        )
        return self.at(slice(None), row, column)

    def _copy(self, source, target, k, device):
        return pltpu.make_async_remote_copy(
            source, target, self.send.at[k], self.recv.at[k], device_id=device, device_id_type=MESH
        )

    def _go(self, *args):
        copy = self._copy(*args)
        copy.start()
        self.started.append(copy)

    def _arrived(self, ref, k):
        self._copy(ref, ref, k, self.to["core"]).wait_recv()

    def start(self):
        far, row, column = self.where
        mine = self.at(far, row, column)
        for k, device in enumerate(self.to["far"]):
            self._go(self.own, mine, k, device)

    def step(self, stage):
        far, row, column = self.where
        near = self._column(())
        if stage == 0:
            count = len(self.to["far"])
            for k in range(count):
                sender = self.to["far_index"][count - 1 - k]
                self._arrived(self.at(sender, row, column), k)
            self._go(near, near, 3, self.to[self.first])
            self._go(near, near, 4, self.to[self.second])
            if self.shared:
                self._go(near, near, 6, self.to["core"])
        if stage == 1:
            got = self._column((self.first,))
            self._arrived(got, 3)
            self._go(got, got, 5, self.to[self.second])
            if self.shared:
                self._go(got, got, 7, self.to["core"])
        if stage == 2:
            for k, names in ((4, (self.second,)), (5, (self.first, self.second))):
                got = self._column(names)
                self._arrived(got, k)
                if self.shared:
                    self._go(got, got, 4 + k, self.to["core"])
        if stage == 3 and self.shared:
            for k, names in enumerate(
                ((), (self.first,), (self.second,), (self.first, self.second))
            ):
                self._arrived(self._other(names), 6 + k)

    def _other(self, names):
        keep, self.at = self.at, self.shared
        ref = self._column(names)
        self.at = keep
        return ref

    def finish(self):
        for copy in self.started:
            copy.wait_send()


class GatherNear(Gather):
    def start(self):
        far, row, column = self.where
        mine = self.at(far, row, column)
        self._go(self.own, mine, 0, self.to[self.first])
        self._go(self.own, mine, 1, self.to[self.second])

    def _near(self, names):
        far, row, column = self.where
        return self.at(
            far, 1 - row if "row" in names else row, 1 - column if "column" in names else column
        )

    def step(self, stage):
        far = self.where[0]
        all_of = slice(None)
        count = len(self.to["far"])
        if stage == 0:
            got = self._near((self.first,))
            self._arrived(got, 0)
            self._go(got, got, 2, self.to[self.second])
        if stage == 1:
            self._arrived(self._near((self.second,)), 1)
            self._arrived(self._near((self.first, self.second)), 2)
            plane = self.at(far, all_of, all_of)
            for k, device in enumerate(self.to["far"]):
                self._go(plane, plane, 3 + k, device)
            if self.shared:
                self._go(plane, plane, 3 + count, self.to["core"])
        if stage == 2:
            for k in range(count):
                plane = self.at(self.to["far_index"][count - 1 - k], all_of, all_of)
                self._arrived(plane, 3 + k)
                if self.shared:
                    self._go(plane, plane, 4 + count + k, self.to["core"])
        if stage == 3 and self.shared:
            self._arrived(self.shared(far, all_of, all_of), 3 + count)
            for k in range(count):
                plane = self.shared(self.to["far_index"][count - 1 - k], all_of, all_of)
                self._arrived(plane, 4 + count + k)


def transposed(left, right):
    return lax.dot_general(left, right, (((0,), (0,)), ((), ())), preferred_element_type=F32)


def against(left, right):
    return lax.dot_general(left, right, (((1,), (1,)), ((), ())), preferred_element_type=F32)


def plain(left, right):
    return lax.dot_general(left, right, (((1,), (0,)), ((), ())), preferred_element_type=F32)


def over_rows(count, tile, work):
    def one(t, carry):
        work(pl.ds(pl.multiple_of(t * tile, tile), tile))
        return carry

    lax.fori_loop(0, count // tile, one, 0)


class Vectors:
    def __init__(self, to, held, arrived, send, recv, order):
        self.to, self.held, self.arrived, self.sems, self.order = to, held, arrived, (send, recv), order
        self.flying, self.slot = [], 0

    def _go(self, k):
        name = self.order[k]
        for device in self.to["far"] if name == "far" else [self.to[name]]:
            slot = self.slot
            copy = pltpu.make_async_remote_copy(
                self.held.at[k], self.arrived.at[slot], self.sems[0].at[slot], self.sems[1].at[slot],
                device_id=device, device_id_type=MESH,
            )
            copy.start()
            self.flying.append((slot, copy))
            self.slot += 1

    def _take(self, k):
        value = self.held[k]
        for slot, copy in self.flying:
            copy.wait()
            value = value + self.arrived[slot]
        self.flying = []
        return value

    def start(self):
        self._go(0)

    def step(self, k):
        self.held[k] = self._take(k - 1)
        self._go(k)

    def result(self):
        return self._take(3)


def attention_forward(pairs, queries, keys, values, valid, probs, mixed, first_lane, turned):
    for pair in range(*pairs):
        lanes = slice(pair * 128, pair * 128 + 128)
        query, key, value = queries[:, lanes] * LOW(HEAD ** (-0.5)), keys[:, lanes], values[:, lanes]
        outs = []
        for j in range(2):
            part = slice(j * HEAD, (j + 1) * HEAD)
            scores = against(key[:, part], query[:, part]) if turned else against(query[:, part], key[:, part])
            if valid is not None:
                scores = jnp.where(lax.broadcasted_iota(jnp.int32, scores.shape, 1) < valid[0, 0], scores, -1e30)
            axis = 0 if turned else 1
            expon = jnp.exp(scores - jnp.max(scores, axis=axis, keepdims=True))
            prob = (expon * (1.0 / jnp.sum(expon, axis=axis, keepdims=True))).astype(LOW)
            probs[pair * 2 + j] = prob
            outs.append((transposed if turned else plain)(prob, value[:, part]))
        mixed[:, pl.ds(pl.multiple_of(first_lane + pair * 128, 128), 128)] = jnp.concatenate(outs, axis=1).astype(LOW)


def norm_parts(values):
    centre = values - jnp.mean(values, axis=-1, keepdims=True)
    factor = lax.rsqrt(jnp.mean(centre * centre, axis=-1, keepdims=True) + epsilon)
    return centre * factor, factor


def norm_backward(unit, factor, gain, delta):
    scaled = delta * gain
    return factor * (scaled - jnp.mean(scaled, axis=-1, keepdims=True) - unit * jnp.mean(scaled * unit, axis=-1, keepdims=True))


def total_rows(values):
    return jnp.sum(values, axis=0, keepdims=True)


def gather_kernel(far_count, proj_in, maps_in, expand_in, shrink_in, bias_in, gain_in, shift_in, shrink_bias_in, expand_bias_in, length,
                  tokens, rows_in, token_cot_in, memory_cot,
                  proj_o, maps_o, expand_o, shrink_o, table_o, hidden_o, middle_full_o, d_branch_x_o,
                  inputs_o, memory_o, qp_o, kp_o, vp_o, qu_o, ku_o, vu_o,
                  probs_p_o, probs_u_o, mixed_p_o, mixed_u_o, packed_o, new_memory_o, middle_sum_o,
                  slope_o, d_sum2_o, d_branch_o, new_tokens_o, d_sum0_o, grad_table_o,
                  inputs, memory, qp, kp, vp, qu, ku, vu, probs_p, probs_u, mixed_p, mixed_u, packed, new_memory, middle_sum,
                  slope, d_sum2, d_branch, new_tokens, d_sum0, grad_table,
                  memory_sum, middle, middle_low, hidden, cot, expand_w, shrink_w,
                  weights, map_p, map_u, token_cot, table, own_vec, vec, vec_all,
                  proj_f, maps_f, expand_f, shrink_f, proj, maps, expand, shrink,
                  send, recv, local, out_sems, cross_send, cross_recv, raw_local, raw_send, raw_recv):
    seq, core = lax.axis_index("seq"), lax.axis_index("mem")
    where = place(seq)
    far, row, column = where
    to = peers(seq, core, far_count)
    wide = maps.shape[-1]
    width = 2 * wide
    own_tokens, own_rows = tokens.shape[0], rows_in.shape[0]

    def cols(which, start=0):
        return pl.ds(pl.multiple_of(which * expand.shape[-1] + start, 128), wide)

    def span(which):
        return pl.ds(pl.multiple_of(which * wide, 128), wide)

    copies, stores = [], []

    def keep(source, target):
        copy = pltpu.make_async_copy(source, target, local.at[len(copies)])
        copy.start()
        copies.append(copy)
        return copy

    def store(source, target):
        copy = pltpu.make_async_copy(source, target, out_sems.at[len(stores)])
        copy.start()
        stores.append(copy)

    own_t = pl.ds(pl.multiple_of(core * own_tokens, 128), own_tokens)
    own_m = pl.ds(pl.multiple_of(core * own_rows, 128), own_rows)
    raw = []
    for n, (source, target) in enumerate(((proj_in, proj_f), (maps_in, maps_f), (expand_in, expand_f), (shrink_in, shrink_f))):
        count, size = source.shape[-2], source.shape[-1] // 2
        place_rows = pl.ds(pl.multiple_of(core * count, 8), count)
        mine, theirs = (pl.ds(pl.multiple_of(which * size, 128), size) for which in (core, 1 - core))
        lead = (slice(None),) * (len(source.shape) - 2)
        raw.append((n, source.at[lead + (slice(None), mine)], source.at[lead + (slice(None), theirs)], target.at[lead + (place_rows,)]))
    for n, own, other, target in raw:
        pltpu.make_async_copy(own, target, raw_local.at[n]).start()
    keep(tokens, inputs.at[own_t])
    keep(rows_in, memory.at[own_m])
    keep(memory_cot, cot.at[own_m])
    keep(token_cot_in, token_cot)
    device = 2 * seq + core
    own_vec[...] = jnp.zeros_like(own_vec)
    for first_row, source in ((0, bias_in), (6, gain_in), (9, shift_in), (12, shrink_bias_in), (16, expand_bias_in)):
        own_vec[first_row : first_row + source.shape[0], 0 : source.shape[1]] = source[...]
    small, large = bias_in.shape[1], expand_bias_in.shape[1]

    def window(start):
        return lax.min(lax.div(start, 128), 2 * wide // 128 - 2)

    offsets = (small * device, lax.rem(large * device, 2 * wide))
    moved = [pltpu.roll(own_vec[k : k + 16 - k // 2], offsets[n] - 128 * window(offsets[n]), 1) for n, k in enumerate((0, 16))]
    vec[...] = jnp.concatenate([moved[0], moved[1], jnp.zeros_like(moved[1])], axis=0).astype(LOW)

    units = []

    def add(first, own, at, shared, kind=Gather):
        k = len(units)
        units.append(kind(where, to, first, own, at, shared, (send.at[k], recv.at[k])))

    def add_proj(first, p):
        add(first, proj.at[p], lambda f, r, c: proj_o.at[p, f, r, c], None)

    def add_map(first, p):
        add(first, maps.at[p], lambda f, r, c: maps_o.at[p, f, r, c, :, span(core)],
            lambda f, r, c: maps_o.at[p, f, r, c, :, span(1 - core)])

    def add_expand(first, k):
        add(first, expand.at[:, pl.ds(k * wide, wide)], lambda f, r, c: expand_o.at[f, r, c, :, cols(core, k * wide)],
            lambda f, r, c: expand_o.at[f, r, c, :, cols(1 - core, k * wide)])

    def add_shrink(first, k):
        rows = shrink.shape[0] // 4
        part = pl.ds(k * rows, rows)
        add(first, shrink.at[part], lambda f, r, c: shrink_o.at[f, r, c, part, span(core)],
            lambda f, r, c: shrink_o.at[f, r, c, part, span(1 - core)], GatherNear if k >= 2 else Gather)

    add("column", vec, lambda f, r, c: vec_all.at[core, f, r, c], lambda f, r, c: vec_all.at[1 - core, f, r, c])
    for first, second in (
        ((add_proj, 0), (add_proj, 1)), ((add_proj, 2), (add_map, 0)), ((add_proj, 4), (add_proj, 5)), ((add_proj, 3), (add_map, 1)),
        ((add_expand, 0), (add_expand, 1)), ((add_expand, 2), (add_expand, 3)), ((add_shrink, 0), (add_shrink, 1)), ((add_shrink, 2), (add_shrink, 3)),
    ):
        first[0]("column", first[1])
        second[0]("row", second[1])

    def cross(k, source, target):
        copy = pltpu.make_async_remote_copy(source, target, cross_send.at[k], cross_recv.at[k], device_id=to["core"], device_id_type=MESH)
        copy.start()
        return copy

    greet(to["far"] + [to["column"], to["row"], to["core"]])
    for n, own, other, target in raw:
        pltpu.make_async_remote_copy(other, target, raw_send.at[n], raw_recv.at[n], device_id=to["core"], device_id_type=MESH).start()
    crossed = [cross(0, tokens, inputs.at[own_t]), cross(1, rows_in, memory.at[own_m]), cross(4, memory_cot, cot.at[own_m])]
    keep(vec, vec_all.at[core, far, row, column])
    units[0].start()
    targets = (
        (proj_f, proj, proj_o.at[:, far, row, column]),
        (maps_f, maps, maps_o.at[:, far, row, column, :, span(core)]),
        (expand_f, expand, expand_o.at[far, row, column, :, pl.ds(pl.multiple_of(core * expand.shape[-1], 128), expand.shape[-1])]),
        (shrink_f, shrink, shrink_o.at[far, row, column, :, span(core)]),
    )
    groups = ((1, 2, 3), (4, 5, 6, 7, 8), (9, 10, 11, 12), (13, 14, 15, 16))
    for (n, own, other, target), (wide_block, block, place_of), group in zip(raw, targets, groups):
        pltpu.make_async_copy(own, target, raw_local.at[n]).wait()
        pltpu.make_async_remote_copy(other, target, raw_send.at[n], raw_recv.at[n], device_id=to["core"], device_id_type=MESH).wait()
        block[...] = wide_block[...].astype(LOW)
        keep(block, place_of)
        for index in group:
            units[index].start()
    for copy in copies:
        copy.wait()
    fetched = {}

    def fetch(key, source, target):
        copy = pltpu.make_async_copy(source, target, local.at[len(copies) + sum(len(v) for v in fetched.values())])
        copy.start()
        fetched.setdefault(key, []).append(copy)

    def need(*keys):
        for key in keys:
            for copy in fetched[key]:
                copy.wait()

    tall = width
    names = ("vec", "p0", "p1", "p2", "m0", "p4", "p5", "p3", "m1", "e0", "e1", "e2", "e3", "s0", "s1", "s2", "s3")

    def complete(name):
        k = int(name[1]) if name != "vec" else 0
        if name[0] == "p":
            fetch(name, proj_o.at[k], weights.at[k])
        elif name[0] == "m":
            fetch(name, maps_o.at[k], (map_p, map_u)[k])
        elif name[0] == "e":
            for side in range(2):
                columns = pl.ds(side * expand.shape[-1] + k * wide, wide)
                fetch(name, expand_o.at[:, :, :, :, columns], expand_w.at[:, :, :, :, columns])
        elif name[0] == "s":
            rows = shrink.shape[0] // 4
            part = pl.ds(k * rows, rows)
            fetch(name, shrink_o.at[:, :, :, part], shrink_w.at[:, :, :, part])

    def weight(p):
        return weights[p].reshape(-1, wide)

    def project(p, source, target, bias):
        need("p" + str(p))

        def one(piece):
            value = plain(source[piece], weight(p))
            if bias is not None:
                value = value + table[bias : bias + 1, span(core)]
            target[piece] = value.astype(LOW)

        one(slice(None))

    def gain(k):
        return table[6 + k : 7 + k]

    def shift(k):
        return table[9 + k : 10 + k]

    def from_other(k, ref):
        copy = pltpu.make_async_remote_copy(ref, ref, cross_send.at[k], cross_recv.at[k], device_id=to["core"], device_id_type=MESH)
        copy.wait_send()
        copy.wait_recv()

    def make_k():
        crossed[0].wait()
        project(1, inputs, kp, None)
        store(inputs, inputs_o)

    def make_q():
        table[...] = jnp.zeros_like(table)
        for k in range(8 * far_count):
            block = vec_all[k % 2, k // 8, (k // 4) % 2, (k // 2) % 2].astype(F32)
            for count, row, start in ((13, 0, small * k), (1, 13 + large * k // width, (large * k) % width)):
                first = 128 * min(start // 128, width // 128 - 2)
                from_row = 0 if count == 13 else 16
                table[row : row + count, first : first + 256] += block[from_row : from_row + count]
        store(table, table_o)
        crossed[1].wait()
        project(0, memory, qp, 0)
        store(memory, memory_o)

    def make_packed():
        from_other(2, mixed_p.at[:, span(core)])
        need("m0")
        for source, target in ((qp, qp_o), (kp, kp_o), (vp, vp_o), (probs_p, probs_p_o), (mixed_p, mixed_p_o)):
            store(source, target)
        value = plain(mixed_p[...], map_p[...].reshape(-1, width)) + table[2:3]
        packed[...] = value.astype(LOW)
        memory_sum[...] = memory[...].astype(F32) + value

    def make_memory():
        crossed[2].wait()
        unit, factor = norm_parts(memory_sum[...])
        memory_sum[...] = unit
        d_sum0[...] = norm_backward(unit, factor, gain(0), cot[...].astype(F32))
        unit, delta = memory_sum[own_m], cot[own_m].astype(F32)
        new_memory[...] = unit * gain(0) + shift(0)
        grad_table[...] = jnp.zeros_like(grad_table)
        grad_table[6:7] = total_rows(delta * unit)
        grad_table[9:10] = total_rows(delta)
        for source, target in ((packed, packed_o), (d_sum0, d_sum0_o), (new_memory, new_memory_o)):
            store(source, target)

    def make_unpack():
        project(4, packed, ku, None)
        project(5, packed, vu, 4)
        store(ku, ku_o)
        store(vu, vu_o)

    sent = []

    def make_middle():
        from_other(3, mixed_u.at[:, span(core)])
        need("m1")
        for source, target in ((qu, qu_o), (probs_u, probs_u_o), (mixed_u, mixed_u_o)):
            store(source, target)

        def attended(t, carry):
            here = pl.ds(pl.multiple_of(t * 256, 256), 256)
            there = pl.ds(pl.multiple_of(core * own_tokens + t * 256, 256), 256)
            value = plain(mixed_u[there], map_u[...].reshape(-1, width)) + table[5:6]
            value = inputs[there].astype(F32) + value
            middle_sum[here] = value
            value = norm_parts(value)[0] * gain(1) + shift(1)
            middle[here] = value
            middle_low[here] = value.astype(LOW)
            return carry

        lax.fori_loop(0, own_tokens // 256, attended, 0)
        store(middle_sum, middle_sum_o)
        store(middle_low, middle_full_o.at[own_t])
        sent.append(cross(5, middle_low, middle_full_o.at[own_t]))

    def widen(n):
        columns = pl.ds(n * tall, tall)
        if n < 2:
            need("e" + str(2 * n), "e" + str(2 * n + 1))
        value = plain(middle_low[...], expand_w[:, :, :, :, columns].reshape(-1, tall)) + table[13 + n : 14 + n]
        share = 0.5 + 0.5 * lax.erf(value * 0.5**0.5)
        hidden[:, columns] = (value * share).astype(LOW)
        slope[:, columns] = (share + value * (0.3989422804014327 * jnp.exp(-0.5 * value * value))).astype(LOW)
        store(hidden.at[:, columns], hidden_o.at[own_t, columns])
        store(slope.at[:, columns], slope_o.at[:, columns])
        sent.append(cross(6 + n, hidden.at[:, columns], hidden_o.at[own_t, columns]))

    def narrow(t, carry):
        here = pl.ds(pl.multiple_of(t * 256, 256), 256)
        value = middle[here] + (plain(hidden[here], shrink_w[...].reshape(-1, width)) + table[12:13])
        unit, factor = norm_parts(value)
        live = core * own_tokens + t * 256 + lax.broadcasted_iota(jnp.int32, (256, 1), 0) < length[0, 0]
        new_tokens[here] = jnp.where(live, unit * gain(2) + shift(2), 0.0)
        delta = jnp.where(live, token_cot[here].astype(F32), 0.0)
        grad_table[8:9] += total_rows(delta * unit)
        grad_table[11:12] += total_rows(delta)
        value = norm_backward(unit, factor, gain(2), delta)
        d_sum2[here] = value
        value = value.astype(LOW)
        d_branch[here] = value
        grad_table[12:13] += total_rows(value.astype(F32))
        return carry

    def make_tokens():
        need("s0", "s1", "s2", "s3")
        lax.fori_loop(0, own_tokens // 256, narrow, 0)
        sent.append(cross(10, d_branch.at[:, span(1 - core)], d_branch_x_o.at[own_t]))
        store(d_branch.at[:, span(core)], d_branch_x_o.at[own_t])
        for source, target in ((d_sum2, d_sum2_o), (d_branch, d_branch_o), (new_tokens, new_tokens_o), (grad_table, grad_table_o)):
            store(source, target)

    work = {
        "k": make_k,
        "q": make_q,
        "v": lambda: project(2, inputs, vp, 1),
        "cx": lambda: cross(2, mixed_p.at[:, span(core)], mixed_p.at[:, span(core)]),
        "yp": make_packed,
        "ln0": make_memory,
        "ku": make_unpack,
        "qu": lambda: project(3, inputs, qu, 3),
        "ux": lambda: cross(3, mixed_u.at[:, span(core)], mixed_u.at[:, span(core)]),
        "att": make_middle,
        "nar": make_tokens,
    }
    for n in range(3):
        work["pf" + str(n)] = functools.partial(attention_forward, (n, n + 1), qp, kp, vp, length, probs_p, mixed_p, core * wide, False)
        work["uf" + str(n)] = functools.partial(attention_forward, (n, n + 1), qu, ku, vu, None, probs_u, mixed_u, core * wide, True)
    for n in range(4):
        work["w" + str(n)] = functools.partial(widen, n)
    for item in FORWARD:
        if isinstance(item, str):
            work[item]()
            continue
        index, stage = item
        units[index].step(stage)
        if stage == (3 if units[index].shared else 2):
            complete(names[index])
    for copy in sent:
        copy.wait()
    for copy in stores:
        copy.wait()
    for unit in units:
        unit.finish()


def gather_chips(far_count, weights, vectors, length, tokens, memory, token_cot, memory_cot):
    grid = (far_count, 2, 2)
    width, hidden = weights[0].shape[-1], weights[2].shape[-1]
    rows, wide = 2 * weights[0].shape[1], width // 2
    blocks = ((6, rows, wide), (2, rows, wide), (rows, hidden // 2), (2 * weights[3].shape[0], wide))
    table = (24, width)
    own_tokens, own_rows = tokens.shape[0], memory.shape[0]
    all_tokens, all_rows = 2 * own_tokens, 2 * own_rows
    count = wide // HEAD
    passed = (
        ((6,) + grid + (rows, wide), LOW),
        ((2,) + grid + (rows, width), LOW),
        (grid + (rows, hidden), LOW),
        (grid + (blocks[3][0], width), LOW),
        (table, F32),
        ((all_tokens, hidden), LOW),
        ((all_tokens, width), LOW),
        ((all_tokens, wide), LOW),
    )
    kept = (
        ((all_tokens, width), LOW),
        ((all_rows, width), LOW),
        ((all_rows, wide), LOW),
        ((all_tokens, wide), LOW),
        ((all_tokens, wide), LOW),
        ((all_tokens, wide), LOW),
        ((all_rows, wide), LOW),
        ((all_rows, wide), LOW),
        ((count, all_rows, all_tokens), LOW),
        ((count, all_rows, all_tokens), LOW),
        ((all_rows, width), LOW),
        ((all_tokens, width), LOW),
        ((all_rows, width), LOW),
        ((own_rows, width), F32),
        ((own_tokens, width), F32),
        ((own_tokens, hidden), LOW),
        ((own_tokens, width), F32),
        ((own_tokens, width), LOW),
        ((own_tokens, width), F32),
        ((all_rows, width), F32),
        (table, F32),
    )
    inner = (
        ((all_rows, width), F32),
        ((own_tokens, width), F32),
        ((own_tokens, width), LOW),
        ((own_tokens, hidden), LOW),
        ((all_rows, width), LOW),
        passed[2],
        passed[3],
        passed[0],
        (passed[1][0][1:], LOW),
        (passed[1][0][1:], LOW),
        ((own_tokens, width), LOW),
        (table, F32),
        ((24, 256), F32),
        ((32, 256), LOW),
        ((2,) + grid + (32, 256), LOW),
    ) + tuple((block, F32) for block in blocks) + tuple((block, LOW) for block in blocks)
    any_space = pl.BlockSpec(memory_space=pl.ANY)
    return pl.pallas_call(
        functools.partial(gather_kernel, far_count),
        out_shape=[jax.ShapeDtypeStruct(*entry) for entry in passed + kept],
        in_specs=[any_space] * 4
        + [pl.BlockSpec(memory_space=pltpu.VMEM)] * 5
        + [pl.BlockSpec(memory_space=pltpu.SMEM)]
        + [any_space] * 4,
        out_specs=[any_space] * (len(passed) + len(kept)),
        scratch_shapes=[pltpu.VMEM(*entry) for entry in kept + inner]
        + [
            pltpu.SemaphoreType.DMA((17, 10)),
            pltpu.SemaphoreType.DMA((17, 10)),
            pltpu.SemaphoreType.DMA((29,)),
            pltpu.SemaphoreType.DMA((36,)),
            pltpu.SemaphoreType.DMA((11,)),
            pltpu.SemaphoreType.DMA((11,)),
            pltpu.SemaphoreType.DMA((4,)),
            pltpu.SemaphoreType.DMA((4,)),
            pltpu.SemaphoreType.DMA((4,)),
        ],
        compiler_params=pltpu.CompilerParams(
            collective_id=0, has_side_effects=True, vmem_limit_bytes=62 << 20
        ),
        name="gather_and_forward",
    )(*weights, *vectors, length, tokens, memory, token_cot, memory_cot)


class Reduce:
    def __init__(self, where, to, first, at, half_in, quarter_in, far_in, sems):
        self.where, self.to, self.at = where, to, at
        self.half_in, self.quarter_in, self.far_in = half_in, quarter_in, far_in
        self.first, self.second = first, ("row" if first == "column" else "column")
        self.send, self.recv = sems

    def _copy(self, source, target, k, device):
        return pltpu.make_async_remote_copy(
            source, target, self.send.at[k], self.recv.at[k], device_id=device, device_id_type=MESH
        )

    def _go(self, *args):
        self._copy(*args).start()

    def _arrived(self, ref, k):
        self._copy(ref, ref, k, self.to["core"]).wait_recv()

    def _column(self, near):
        far, row, column = self.where
        row, column = (
            (1 - row if "row" in near else row),
            (1 - column if "column" in near else column),
        )
        return self.at(slice(None), row, column)

    def start(self):
        for k, names in ((1, (self.first, self.second)), (0, (self.second,))):
            self._go(self._column(names), self.half_in.at[k], k, self.to[self.second])

    def _add(self, target, other):
        for k in range(target.shape[0]):
            target[k] = (target[k].astype(F32) + other[k].astype(F32)).astype(LOW)

    def step(self, stage):
        count = len(self.to["far"])
        own, near = self._column(()), self._column((self.first,))
        if stage == 0:
            self.start()
        if stage == 1:
            self._arrived(self.half_in.at[1], 1)
            self._add(near, self.half_in.at[1])
            self._go(near, self.quarter_in, 2, self.to[self.first])
        if stage == 2:
            self._arrived(self.half_in.at[0], 0)
            self._add(own, self.half_in.at[0])
        if stage == 3:
            self._arrived(self.quarter_in, 2)
            self._add(own, self.quarter_in)
            for k, device in enumerate(self.to["far"]):
                self._go(own.at[self.to["far_index"][k]], self.far_in.at[k], 3 + k, device)
        if stage == 4:
            for k in range(count):
                self._arrived(self.far_in.at[k], 3 + k)

    def result(self):
        value = self._column(())[self.where[0]].astype(F32)
        for k in range(len(self.to["far"])):
            value = value + self.far_in[k].astype(F32)
        return value

    def finish(self):
        refs = [self.half_in.at[0], self.half_in.at[1], self.quarter_in]
        refs += [self.far_in.at[k] for k in range(len(self.to["far"]))]
        for k, ref in enumerate(refs):
            self._copy(ref, ref, k, self.to["core"]).wait_send()


def attention_backward(pairs, queries, keys, values, probs, mixed, d_query, d_key, d_value, turned):
    scale = HEAD ** (-0.5)
    for pair in range(*pairs):
        lanes = slice(pair * 128, pair * 128 + 128)
        query, delta = queries[:, lanes], mixed[:, lanes]
        key, value = keys[:, lanes], values[:, lanes]
        by_query, by_key = (transposed, plain) if turned else (plain, transposed)
        parts = ([], [], [])
        for j in range(2):
            part = slice(j * HEAD, (j + 1) * HEAD)
            prob_low = probs[pair * 2 + j]
            prob = prob_low.astype(F32)
            d_prob = against(value[:, part], delta[:, part]) if turned else against(delta[:, part], value[:, part])
            row_delta = jnp.sum(d_prob * prob, axis=0 if turned else 1, keepdims=True)
            d_score = (prob * (d_prob - row_delta)).astype(LOW)
            parts[0].append(by_query(d_score, key[:, part]))
            parts[1].append(by_key(d_score, query[:, part]))
            parts[2].append(by_key(prob_low, delta[:, part]))
        d_query[:, lanes] = (jnp.concatenate(parts[0], axis=1) * scale).astype(LOW)
        d_key[:, lanes] = (jnp.concatenate(parts[1], axis=1) * scale).astype(LOW)
        d_value[:, lanes] = jnp.concatenate(parts[2], axis=1).astype(LOW)


def reduce_kernel(far_count, table, vectors_in, hidden_h, d_branch_x_h, d_branch_h, slope_h, expand_h, shrink_h, middle_h, d_sum2_h, middle_sum_h,
                  mixed_u_h, mixed_p_h, inputs_h, memory_h, qu_h, ku_h, vu_h, qp_h, kp_h, vp_h, probs_u_h, probs_p_h, packed_h, d_sum0_h, proj_h, maps_h,
                  proj_o, maps_o, expand_o, shrink_o, vec_o, tokens_o, memory_o,
                  half_in, quarter_in, far_in, vec_sum, vec_in, sums,
                  grads, expand_grads, shrink_grads, d_hidden_x, d_unpacked, d_sum1, partial, partial_in, wide_out, wide_in, rows_out, rows_in,
                  send, recv, last_send, last_recv, last_local, in_sems, cross_send, cross_recv, vec_send, vec_recv):
    seq, core = lax.axis_index("seq"), lax.axis_index("mem")
    where = place(seq)
    to = peers(seq, core, far_count)
    wide = proj_h.shape[-1]
    width = 2 * wide
    rows = proj_o.shape[-2] * 2
    part = rows // 2
    own_rows = d_sum1.shape[0]
    mem_rows = packed_h.shape[0] // 2
    units, ends = [], []

    def span(which, start=0, whole=None):
        return pl.ds(pl.multiple_of(which * (whole or wide) + start, 128), wide)

    loads = {}

    def fetch(name, source, target):
        loads[name] = (source, target, len(loads))
        pltpu.make_async_copy(source, target, in_sems.at[len(loads) - 1]).start()

    def need(*names):
        for name in names:
            source, target, index = loads[name]
            pltpu.make_async_copy(source, target, in_sems.at[index]).wait()

    def below(refs):
        for name, source, target in refs:
            fetch(name, source, target)

    fetch("vectors", vectors_in, vec_sum.at[0])

    def add(at, end):
        k = len(units)
        first = "column" if k % 2 == 0 else "row"
        units.append(Reduce(where, to, first, at, half_in.at[k], quarter_in.at[k], far_in.at[k], (send.at[k], recv.at[k])))
        ends.append(end)

    def add_expand(k):
        add(lambda f, r, c: expand_grads.at[k, f, r, c],
            lambda which: expand_o.at[:, span(which, k * wide, expand_o.shape[-1] // 2)])

    def add_shrink(k):
        add(lambda f, r, c: shrink_grads.at[f, r, c, pl.ds(k * rows, rows)], None)

    def add_map(p):
        add(lambda f, r, c: grads.at[6 + p, f, r, c], lambda which: maps_o.at[p, :, span(which)])

    def add_proj(p):
        add(lambda f, r, c: grads.at[p, f, r, c], lambda which: proj_o.at[p, :, span(which)])

    for k in range(4):
        add_shrink(k)
    for k in range(4):
        add_expand(k)
    for make, p in ((add_map, 1), (add_proj, 3), (add_proj, 4), (add_proj, 5), (add_map, 0), (add_proj, 0), (add_proj, 1), (add_proj, 2)):
        make(p)

    bias_sums = Vectors(to, vec_sum, vec_in, vec_send, vec_recv, ("core", "column", "row", "far"))

    def last(k, source, target):
        return pltpu.make_async_remote_copy(source, target, last_send.at[k], last_recv.at[k], device_id=to["core"], device_id_type=MESH)

    def close(k, start):
        if ends[k] is None:
            owner = k // 2
            row = pl.ds((k % 2) * rows, rows)

            @pl.when(core == owner)
            def _():
                local = pltpu.make_async_copy(sums.at[k], shrink_o.at[row, span(core)], last_local.at[k])
                if start:
                    local.start()
                else:
                    local.wait()
                    last(k, sums.at[k], shrink_o.at[row, span(1 - core)]).wait_recv()

            @pl.when(core != owner)
            def _():
                copy = last(k, sums.at[k], shrink_o.at[row, span(core)])
                if start:
                    copy.start()
                else:
                    copy.wait_send()

            return
        own = sums.at[k, pl.ds(pl.multiple_of(core * part, 8), part)]
        other = sums.at[k, pl.ds(pl.multiple_of((1 - core) * part, 8), part)]
        local = pltpu.make_async_copy(own, ends[k](core), last_local.at[k])
        copy = last(k, other, ends[k](core))
        if start:
            local.start()
            copy.start()
        else:
            local.wait()
            copy.wait_send()
            last(k, ends[k](1 - core), ends[k](1 - core)).wait_recv()

    place_in_plan = [0]

    def turn(name):
        while place_in_plan[0] < len(BACKWARD):
            item = BACKWARD[place_in_plan[0]]
            place_in_plan[0] += 1
            if isinstance(item, str):
                if item != name:
                    raise ValueError(item)
                return
            index, stage = item
            if index == 16:
                if stage == 0:
                    bias_sums.start()
                elif stage < 4:
                    bias_sums.step(stage)
                else:
                    vec_o[...] = bias_sums.result()
                continue
            units[index].step(stage)
            if stage == 4:
                sums[index] = units[index].result()
                close(index, True)

    def weight_grad(slots, left, *rights):
        right = rights[0] if len(rights) == 1 else jnp.concatenate(rights, axis=1)
        value = transposed(left[...], right).astype(LOW)
        for k, slot in enumerate(slots):
            grads[slot] = value[:, k * wide : (k + 1) * wide].reshape(grads.shape[1:])

    def put_bias(row, values):
        vec_sum[0, row : row + 1, span(core)] = jnp.sum(values.astype(F32), axis=0, keepdims=True)

    def cross(k, source, target):
        copy = pltpu.make_async_remote_copy(source, target, cross_send.at[k], cross_recv.at[k], device_id=to["core"], device_id_type=MESH)
        copy.start()
        return copy

    hidden = hidden_h.shape[1]
    quarter = hidden // 4
    own = pl.ds(pl.multiple_of(core * own_rows, 128), own_rows)
    other = pl.ds(pl.multiple_of((1 - core) * own_rows, 128), own_rows)

    def shrink_gradient(tiles, d_branch_x, d_branch, shrink_w, slope, middle):
        below((("d_branch_x", d_branch_x_h, d_branch_x),))
        ready = []
        for n in range(4):
            copy = pltpu.make_async_copy(hidden_h.at[:, pl.ds(n * quarter, quarter)], tiles.at[n % 2], in_sems.at[30 + n])
            ready.append(copy)
        ready[0].start()
        ready[1].start()
        below((("d_branch", d_branch_h, d_branch), ("shrink", shrink_h, shrink_w), ("slope", slope_h, slope), ("middle", middle_h, middle)))
        tall = shrink_grads.shape[3]
        greet(to["far"] + [to["column"], to["row"], to["core"]])
        need("d_branch_x")
        for n in range(4):
            ready[n].wait()
            value = transposed(tiles[n % 2], d_branch_x[...]).astype(LOW)
            for b in range(quarter // tall):
                block = n * (quarter // tall) + b
                shrink_grads[block // 4, (block // 2) % 2, block % 2] = value[b * tall : (b + 1) * tall]
            if n + 2 < 4:
                ready[n + 2].start()
        need("d_branch", "shrink", "slope", "vectors")
        sent = []
        for k in range(4):
            if k % 2 == 0:
                turn("dha" if k == 0 else "dhb")
            which = 1 - core if k < 2 else core
            piece = which * 2 + k % 2
            columns = pl.ds(pl.multiple_of(piece * quarter, 128), quarter)
            here = pl.ds((k % 2) * quarter, quarter)
            value = against(d_branch[...], shrink_w[pl.ds(piece * (quarter // tall), quarter // tall)].reshape(quarter, width))
            value = (value * slope[:, columns].astype(F32)).astype(LOW)
            slope[:, columns] = value
            vec_sum[0, pl.ds(13 + piece, 1), :] = total_rows(value.astype(F32))
            if k < 2:
                sent.append(cross(3 + k, slope.at[:, columns], d_hidden_x.at[own, here]))
            else:
                d_hidden_x[own, here] = value
        for copy in sent:
            copy.wait()

    def expand_gradient(expand_w, d_sum2, middle_sum, d_hidden, middle):
        below((("expand", expand_h, expand_w), ("d_sum2", d_sum2_h, d_sum2), ("middle_sum", middle_sum_h, middle_sum)))
        need("middle")

        def one(k):
            value = transposed(middle[...], d_hidden_x[:, k * width : (k + 1) * width]).astype(LOW)
            for j in range(2):
                expand_grads[2 * k + j] = value[:, j * wide : (j + 1) * wide].reshape(expand_grads.shape[1:])

        turn("de0")
        one(0)
        turn("de1")
        one(1)
        need("expand", "d_sum2", "middle_sum")
        vec_sum[0, 5:6] = jnp.zeros((1, width), F32)
        vec_sum[0, 7:8] = jnp.zeros((1, width), F32)
        vec_sum[0, 10:11] = jnp.zeros((1, width), F32)

        def two(t, carry):
            here = pl.ds(pl.multiple_of(t * 256, 256), 256)
            delta = d_sum2[here] + against(d_hidden[here], expand_w[...].reshape(width, hidden))
            unit, factor = norm_parts(middle_sum[here])
            vec_sum[0, 7:8] += total_rows(delta * unit)
            vec_sum[0, 10:11] += total_rows(delta)
            delta = norm_backward(unit, factor, table[7:8], delta)
            d_sum1[here] = delta
            low = delta.astype(LOW)
            d_unpacked[pl.ds(pl.multiple_of(core * own_rows + t * 256, 256), 256)] = low
            vec_sum[0, 5:6] += total_rows(low.astype(F32))
            return carry

        turn("dm0")
        lax.fori_loop(0, own_rows // 512, two, 0)
        turn("dm1")
        lax.fori_loop(own_rows // 512, own_rows // 256, two, 0)
        return cross(5, d_unpacked.at[own], d_unpacked.at[own])

    def feed_forward(slope, middle):
        like = lambda ref: pltpu.VMEM(ref.shape, ref.dtype)
        pl.run_scoped(
            lambda *refs: shrink_gradient(*refs, slope, middle),
            pltpu.VMEM((2, hidden_h.shape[0], quarter), LOW), like(d_branch_x_h), like(d_branch_h), like(shrink_h),
        )
        pl.run_scoped(
            lambda *refs: expand_gradient(*refs, slope, middle).wait(),
            like(expand_h), like(d_sum2_h), like(middle_sum_h),
        )

    pl.run_scoped(feed_forward, pltpu.VMEM(slope_h.shape, LOW), pltpu.VMEM(middle_h.shape, LOW))

    def attention(map_u, map_p, mixed_u, mixed_p, inputs, memory, qu, ku, vu, qp, kp, vp, probs, packed, d_sum0, weights,
                  d_mixed, d_query, d_key, d_value, d_token_key, d_token_value, d_packed):
        mine = pl.ds(pl.multiple_of(core * wide, 128), wide)
        below((
            ("map_u", maps_h.at[1, mine], map_u), ("mixed_u", mixed_u_h, mixed_u), ("qu", qu_h, qu), ("ku", ku_h, ku), ("vu", vu_h, vu), ("probs_u", probs_u_h, probs),
            ("inputs", inputs_h, inputs), ("packed", packed_h, packed), ("weights", proj_h, weights), ("d_sum0", d_sum0_h, d_sum0),
            ("map_p", maps_h.at[0, mine], map_p), ("mixed_p", mixed_p_h, mixed_p), ("qp", qp_h, qp), ("kp", kp_h, kp), ("vp", vp_h, vp), ("memory", memory_h, memory),
        ))
        need("map_u")

        def from_map_u(piece):
            d_mixed[piece] = against(d_unpacked[piece], map_u[...]).astype(LOW)

        turn("mix")
        from_map_u(slice(None))
        need("mixed_u")
        turn("gm1")
        weight_grad((7,), mixed_u, d_unpacked[:, span(core)])
        need("qu", "ku", "vu", "probs_u")
        for n in range(3):
            turn("ua" + str(n))
            attention_backward((n, n + 1), qu, ku, vu, probs, d_mixed, d_query, d_key, d_value, True)
        below((("probs_p", probs_p_h, probs),))
        need("inputs", "packed", "weights", "d_sum0")
        turn("pk")
        partial[...] = against(d_key[...], weights[4]) + against(d_value[...], weights[5])
        packing = cross(0, partial, partial_in)
        turn("g3")
        weight_grad((3,), inputs, d_query[...])
        turn("g45")
        weight_grad((4, 5), packed, d_key[...], d_value[...])
        put_bias(3, d_query[...])
        put_bias(4, d_value[...])

        turn("gm0")
        packing.wait()
        d_packed[...] = (d_sum0[...] + (partial[...] + partial_in[...])).astype(LOW)
        need("map_p", "mixed_p")
        d_mixed_p = d_mixed.at[pl.ds(0, 2 * mem_rows)]
        d_mixed_p[...] = against(d_packed[...], map_p[...]).astype(LOW)
        weight_grad((6,), mixed_p, d_packed[:, span(core)])
        vec_sum[0, 2:3, :] = total_rows(d_packed[pl.ds(pl.multiple_of(core * mem_rows, 128), mem_rows)].astype(F32))
        need("qp", "kp", "vp", "probs_p")
        for n in range(3):
            turn("pa" + str(n))
            attention_backward((n, n + 1), qp, kp, vp, probs, d_mixed_p, d_key, d_token_key, d_token_value, False)
        need("memory")
        turn("g0")
        weight_grad((0,), memory, d_key[...])
        turn("g12")
        weight_grad((1, 2), inputs, d_token_key[...], d_token_value[...])
        put_bias(0, d_key[...])
        put_bias(1, d_token_value[...])
        turn("tok0")
        own_mem = pl.ds(pl.multiple_of(core * mem_rows, 128), mem_rows)
        other_mem = pl.ds(pl.multiple_of((1 - core) * mem_rows, 128), mem_rows)
        rows_out[...] = against(d_key[...], weights[0])
        memory_terms = cross(2, rows_out.at[other_mem], rows_in)
        wide_out[...] = against(d_query[other], weights[3]) + against(d_token_key[other], weights[1]) + against(d_token_value[other], weights[2])
        token_terms = cross(1, wide_out, wide_in)
        turn("out0")
        tokens_o[...] = d_sum1[...] + against(d_query[own], weights[3])
        turn("out1")
        tokens_o[...] = tokens_o[...] + against(d_token_key[own], weights[1]) + against(d_token_value[own], weights[2])
        turn("fin")
        memory_terms.wait()
        memory_o[...] = d_sum0[own_mem] + rows_out[own_mem] + rows_in[...]
        token_terms.wait()
        tokens_o[...] = tokens_o[...] + wide_in[...]
        turn(None)
        for k in range(len(units)):
            close(k, False)
        for unit in units:
            unit.finish()

    like = lambda ref: pltpu.VMEM(ref.shape, ref.dtype)
    tokens, memories = like(qu_h), like(ku_h)
    pl.run_scoped(
        attention,
        pltpu.VMEM((wide, width), LOW), pltpu.VMEM((wide, width), LOW), like(mixed_u_h), like(mixed_p_h), like(inputs_h), like(memory_h),
        tokens, memories, memories, memories, tokens, tokens, like(probs_u_h), like(packed_h), like(d_sum0_h), like(proj_h),
        tokens, tokens, memories, memories, tokens, tokens, like(packed_h),
    )


def reduce_chips(far_count, table, vectors, arrays):
    hidden_full, slope, d_sum2, inputs, memory = arrays[0], arrays[3], arrays[7], arrays[11], arrays[12]
    proj = arrays[-2]
    rows, wide = proj.shape[1] // (4 * far_count), proj.shape[2]
    part, width, hidden = rows // 2, 2 * wide, hidden_full.shape[1]
    all_tokens, own_tokens, all_rows = inputs.shape[0], slope.shape[0], memory.shape[0]
    grid = (far_count, 2, 2)
    any_space = pl.BlockSpec(memory_space=pl.ANY)
    vmem = pl.BlockSpec(memory_space=pltpu.VMEM)
    shapes = ((6, part, width), (2, part, width), (part, hidden), (hidden // (8 * far_count), width), vectors.shape, d_sum2.shape, (all_rows // 2, width))
    return pl.pallas_call(
        functools.partial(reduce_kernel, far_count),
        out_shape=[jax.ShapeDtypeStruct(shape, F32) for shape in shapes],
        in_specs=[vmem] + [any_space] * (1 + len(arrays)),
        out_specs=[vmem] * 7,
        scratch_shapes=[
            pltpu.VMEM((16, 2, far_count, rows, wide), LOW),
            pltpu.VMEM((16, far_count, rows, wide), LOW),
            pltpu.VMEM((16, far_count - 1, rows, wide), LOW),
            pltpu.VMEM((4,) + vectors.shape, F32),
            pltpu.VMEM((2 + far_count,) + vectors.shape, F32),
            pltpu.VMEM((16, rows, wide), F32),
            pltpu.VMEM((8,) + grid + (rows, wide), LOW),
            pltpu.VMEM((4,) + grid + (rows, wide), LOW),
            pltpu.VMEM(grid + (hidden // (4 * far_count), wide), LOW),
            pltpu.VMEM((all_tokens, hidden // 2), LOW),
            pltpu.VMEM((all_tokens, width), LOW),
            pltpu.VMEM((own_tokens, width), F32),
            pltpu.VMEM((all_rows, width), F32),
            pltpu.VMEM((all_rows, width), F32),
            pltpu.VMEM((own_tokens, width), F32),
            pltpu.VMEM((own_tokens, width), F32),
            pltpu.VMEM((all_rows, width), F32),
            pltpu.VMEM((all_rows // 2, width), F32),
            pltpu.SemaphoreType.DMA((16, 6)),
            pltpu.SemaphoreType.DMA((16, 6)),
            pltpu.SemaphoreType.DMA((16,)),
            pltpu.SemaphoreType.DMA((16,)),
            pltpu.SemaphoreType.DMA((16,)),
            pltpu.SemaphoreType.DMA((34,)),
            pltpu.SemaphoreType.DMA((6,)),
            pltpu.SemaphoreType.DMA((6,)),
            pltpu.SemaphoreType.DMA((2 + far_count,)),
            pltpu.SemaphoreType.DMA((2 + far_count,)),
        ],
        compiler_params=pltpu.CompilerParams(
            collective_id=1, has_side_effects=True, vmem_limit_bytes=62 << 20
        ),
        name="backward_and_sums",
    )(table, vectors, *arrays)


def deliver_kernel(count, *refs):
    sources, table, targets, vectors = refs[:count], refs[count], refs[count + 1 : 2 * count + 1], refs[2 * count + 1 : 2 * count + 6]
    held, sems = refs[2 * count + 6 : 3 * count + 6], refs[3 * count + 6]
    loads = [pltpu.make_async_copy(source, hold, sems.at[0, k]) for k, (source, hold) in enumerate(zip(sources, held))]
    stores = [pltpu.make_async_copy(hold, target, sems.at[1, k]) for k, (hold, target) in enumerate(zip(held, targets))]
    for copy in loads:
        copy.start()
    device = 2 * lax.axis_index("seq") + lax.axis_index("mem")
    width = table.shape[1]
    small, large = vectors[0].shape[1], vectors[3].shape[1]
    turned = pltpu.roll(table[0:16], lax.rem(width - small * device, width), 1)[:, 0:small]
    vectors[0][...] = turned[0:6]
    vectors[1][...] = turned[6:9]
    vectors[2][...] = turned[9:12]
    vectors[4][...] = turned[12:13]
    row, column = lax.div(large * device, width), lax.rem(large * device, width)
    vectors[3][...] = pltpu.roll(table[pl.ds(13 + row, 1)], lax.rem(width - column, width), 1)[:, 0:large]
    for load, copy in zip(loads, stores):
        load.wait()
        copy.start()
    for copy in stores:
        copy.wait()


def deliver(arrays, table, part, count):
    any_space, vmem = pl.BlockSpec(memory_space=pl.ANY), pl.BlockSpec(memory_space=pltpu.VMEM)
    shapes = [array.shape for array in arrays] + [(6, part), (3, part), (3, part), (1, count), (1, part)]
    return pl.pallas_call(
        functools.partial(deliver_kernel, len(arrays)),
        out_shape=[jax.ShapeDtypeStruct(shape, F32) for shape in shapes],
        in_specs=[any_space] * len(arrays) + [vmem],
        out_specs=[any_space] * len(arrays) + [vmem] * 5,
        scratch_shapes=[pltpu.VMEM(array.shape, F32) for array in arrays] + [pltpu.SemaphoreType.DMA((2, len(arrays)))],
        compiler_params=pltpu.CompilerParams(vmem_limit_bytes=62 << 20),
        name="deliver",
    )(*arrays, table)


def norm_apply(values, gain, shift):
    centre = values - jnp.mean(values, axis=-1, keepdims=True)
    spread = jnp.mean(centre * centre, axis=-1, keepdims=True)
    return centre * lax.rsqrt(spread + epsilon) * gain + shift


def gelu_exact(values):
    return jax.nn.gelu(values, approximate=False)


def heads_of(values):
    return values.reshape(values.shape[0], values.shape[1] // HEAD, HEAD)


def scores_of(queries, keys, valid):
    scores = jnp.einsum(
        "rhd,chd->hrc", heads_of(queries), heads_of(keys), preferred_element_type=F32
    ) * HEAD ** (-0.5)
    if valid is not None:
        scores = jnp.where(valid[None, None, :], scores, -1e30)
    return scores


def attend_forward(queries, keys, values, valid):
    scores = scores_of(queries, keys, valid)
    top = jnp.max(scores, axis=-1, keepdims=True)
    expon = jnp.exp(scores - top)
    total = jnp.sum(expon, axis=-1, keepdims=True)
    probs = to_low(expon / total)
    mixed = jnp.einsum("hrc,chd->rhd", probs, heads_of(values), preferred_element_type=F32)
    return to_low(mixed.reshape(queries.shape)), top + jnp.log(total), probs


def attend_backward(queries, keys, values, valid, log_total, delta_mixed):
    probs = jnp.exp(scores_of(queries, keys, valid) - log_total)
    delta_heads = heads_of(delta_mixed)
    delta_values = jnp.einsum("hrc,rhd->chd", to_low(probs), delta_heads, preferred_element_type=F32)
    delta_probs = jnp.einsum("rhd,chd->hrc", delta_heads, heads_of(values), preferred_element_type=F32)
    row_delta = jnp.sum(delta_probs * probs, axis=-1, keepdims=True)
    score_low = to_low(probs * (delta_probs - row_delta))
    scale = HEAD ** (-0.5)
    delta_query = jnp.einsum("hrc,chd->rhd", score_low, heads_of(keys), preferred_element_type=F32) * scale
    delta_keys = jnp.einsum("hrc,rhd->chd", score_low, heads_of(queries), preferred_element_type=F32) * scale
    return (
        to_low(delta_query.reshape(queries.shape)),
        to_low(delta_keys.reshape(keys.shape)),
        to_low(delta_values.reshape(keys.shape)),
    )


def body(
    custom,
    tokens,
    memory,
    lengths,
    tokens_cotangent,
    memory_cotangent,
    projections,
    output_maps,
    expand_weight,
    shrink_weight,
    projection_bias,
    norm_gain,
    norm_bias,
    expand_bias,
    shrink_bias,
):
    share = lax.axis_index("mem")
    chips = lax.axis_size("seq")
    width = tokens.shape[1]
    hidden = expand_weight.shape[1]
    part = projections.shape[1]
    rows = 2 * part

    def block(values, axis):
        low = to_low(values)
        wide = axis + 1
        return join(half(low, share, wide), swap(half(low, 1 - share, wide)), axis)

    own_count = tokens.shape[0]
    device = 2 * lax.axis_index("seq") + share
    if custom:
        (
            proj_all, maps_all, expand_mat, shrink_mat, table, hidden_full, middle_full, d_branch_x, inputs, rows_all, pack_query, pack_keys,
            pack_values, unpack_query, unpack_keys, unpack_values, pack_probs, unpack_probs, pack_mixed, unpack_mixed, packed_low, new_memory,
            middle_sum, slope, delta_sum2, delta_branch, new_tokens, delta_sum0, vectors,
        ) = gather_chips(
            chips // 4,
            (projections, output_maps, expand_weight, shrink_weight),
            (projection_bias, norm_gain, norm_bias, shrink_bias[None], expand_bias[None]),
            lengths[None], tokens, memory, tokens_cotangent, memory_cotangent,
        )
        proj_all = proj_all.reshape(6, width, width // 2)
        maps_all = maps_all.reshape(2, width, width)
        shrink_mat = shrink_mat.reshape(chips, hidden // chips, width)
        proj_o, maps_o, expand_o, shrink_o, vec_o, tokens_grad, memory_grad = reduce_chips(
            chips // 4,
            table,
            vectors,
            (
                hidden_full, d_branch_x, delta_branch, slope, expand_mat, shrink_mat, middle_full, delta_sum2, middle_sum,
                unpack_mixed, pack_mixed, inputs, rows_all, unpack_query, unpack_keys, unpack_values,
                pack_query, pack_keys, pack_values, unpack_probs, pack_probs, packed_low, delta_sum0, proj_all, maps_all,
            ),
        )
        results = deliver(
            (new_tokens, new_memory, tokens_grad, memory_grad, proj_o, maps_o, expand_o, shrink_o), vec_o, part, hidden // (2 * chips)
        )
        return tuple(results[:11]) + (results[11][0], results[12][0])
    else:
        vectors = [to_low(v).astype(F32) for v in (projection_bias, norm_gain, norm_bias, shrink_bias[None], expand_bias)]
        blocks = (block(projections, 1), block(output_maps, 1), block(expand_weight, 0), block(shrink_weight, 0))
        length = lengths[0]
        own_valid = share * own_count + jnp.arange(own_count) < length
        all_valid = jnp.arange(2 * own_count) < length
        gather = lambda values, axis: lax.all_gather(values, "seq", axis=axis, tiled=True)
        proj_all = gather(blocks[0], 1)
        maps_all = both(gather(blocks[1], 1), 2)
        expand_mat = both(gather(blocks[2], 0), 1)
        shrink_mat = both(gather(blocks[3], 0), 1)
        table = lax.all_gather(jnp.concatenate(vectors[:4]), AXES, axis=1, tiled=True)
        line = lax.all_gather(vectors[4], AXES, axis=0, tiled=True)
        table = jnp.concatenate([table, line.reshape(-1, width)])
        biases, gains, shifts, shrink_shift = table[0:6], table[6:9], table[9:12], table[12]
        expand_shift = table[13 : 13 + hidden // width].reshape(hidden)
        bias_half = half(biases, share, 1)
        inputs, rows_all, memory_cot = both(tokens), both(memory), both(memory_cotangent)
        pack_query = to_low(matmul(rows_all, proj_all[0]) + bias_half[0])
        pack_keys = to_low(matmul(inputs, proj_all[1]))
        pack_values = to_low(matmul(inputs, proj_all[2]) + bias_half[1])
        pack_own, pack_total, pack_probs = attend_forward(pack_query, pack_keys, pack_values, all_valid)
        pack_mixed = both(pack_own, 1)
        packed = matmul(pack_mixed, maps_all[0]) + biases[2]
        packed_low = to_low(packed)
        memory_sum = rows_all.astype(F32) + packed
        new_memory = norm_apply(half(memory_sum, share, 0), gains[0], shifts[0])
        unpack_keys = to_low(matmul(packed_low, proj_all[4]))
        unpack_values = to_low(matmul(packed_low, proj_all[5]) + bias_half[4])
        unpack_query = to_low(matmul(inputs, proj_all[3]) + bias_half[3])
        unpack_own, unpack_total, unpack_probs = attend_forward(unpack_query, unpack_keys, unpack_values, None)
        unpack_mixed = both(unpack_own, 1)
        middle_sum = tokens.astype(F32) + matmul(half(unpack_mixed, share, 0), maps_all[1]) + biases[5]
        middle = norm_apply(middle_sum, gains[1], shifts[1])
        middle_low = to_low(middle)
        hidden_in = matmul(middle_low, expand_mat) + expand_shift
        hidden_low = to_low(gelu_exact(hidden_in))
        output_sum = middle + matmul(hidden_low, shrink_mat) + shrink_shift
        layer_out = norm_apply(output_sum, gains[2], shifts[2])
        new_tokens = jnp.where(own_valid[:, None], layer_out, 0.0)

        delta_out = jnp.where(own_valid[:, None], tokens_cotangent.astype(F32), 0.0)
        dropped, norm_back = jax.vjp(norm_apply, output_sum, gains[2], shifts[2])
        delta_sum2, delta_gain2, delta_shift2 = norm_back(delta_out)
        delta_branch = to_low(delta_sum2)
        delta_hidden = matmul_right(delta_branch, shrink_mat)
        dropped, gelu_back = jax.vjp(gelu_exact, hidden_in)
        delta_hidden_in = to_low(gelu_back(delta_hidden)[0])
        delta_shrink = matmul_left(
            both(hidden_low), join(half(delta_branch, share, 1), swap(half(delta_branch, 1 - share, 1)))
        )
        delta_expand = matmul_left(
            both(middle_low), join(half(delta_hidden_in, share, 1), swap(half(delta_hidden_in, 1 - share, 1)))
        )
        delta_middle = delta_sum2 + matmul_right(delta_hidden_in, expand_mat)
        dropped, norm_back = jax.vjp(norm_apply, middle_sum, gains[1], shifts[1])
        delta_sum1, delta_gain1, delta_shift1 = norm_back(delta_middle)
        delta_own = to_low(delta_sum1)
        delta_unpacked = both(delta_own)
        dropped, norm_back = jax.vjp(norm_apply, memory_sum, gains[0], shifts[0])
        delta_sum0 = norm_back(memory_cot.astype(F32))[0]
        dropped, norm_back = jax.vjp(norm_apply, half(memory_sum, share, 0), gains[0], shifts[0])
        dropped, delta_gain0, delta_shift0 = norm_back(memory_cotangent.astype(F32))
        known = [delta_gain0, delta_gain1, delta_gain2, delta_shift0, delta_shift1, delta_shift2, column_sum(delta_branch)]
        delta_map1 = matmul_left(unpack_mixed, half(delta_unpacked, share, 1))
        delta_mixed = to_low(matmul_right(delta_unpacked, half(maps_all[1], share, 0)))
        delta_uquery, delta_ukeys, delta_uvalues = attend_backward(
            unpack_query, unpack_keys, unpack_values, None, unpack_total, delta_mixed
        )
        delta_proj3 = matmul_left(inputs, delta_uquery)
        delta_proj4 = matmul_left(packed_low, delta_ukeys)
        delta_proj5 = matmul_left(packed_low, delta_uvalues)
        partial = matmul_right(delta_ukeys, proj_all[4]) + matmul_right(delta_uvalues, proj_all[5])
        delta_packed = to_low(delta_sum0 + (partial + swap(partial)))
        delta_map0 = matmul_left(pack_mixed, half(delta_packed, share, 1))
        delta_mixed = to_low(matmul_right(delta_packed, half(maps_all[0], share, 0)))
        delta_pquery, delta_pkeys, delta_pvalues = attend_backward(
            pack_query, pack_keys, pack_values, all_valid, pack_total, delta_mixed
        )
        delta_proj0 = matmul_left(rows_all, delta_pquery)
        delta_proj1 = matmul_left(inputs, delta_pkeys)
        delta_proj2 = matmul_left(inputs, delta_pvalues)
        partial = matmul_right(delta_pquery, proj_all[0])
        memory_grad = half(delta_sum0, share, 0) + half(partial, share, 0) + swap(half(partial, 1 - share, 0))
        partial = (
            matmul_right(delta_uquery, proj_all[3])
            + matmul_right(delta_pkeys, proj_all[1])
            + matmul_right(delta_pvalues, proj_all[2])
        )
        tokens_grad = delta_sum1 + half(partial, share, 0) + swap(half(partial, 1 - share, 0))

        zero = jnp.zeros((1, width // 2), F32)

        def spread(values):
            return join(values, zero[0])

        bias_grads = [
            spread(column_sum(delta_pquery)),
            spread(column_sum(delta_pvalues)),
            column_sum(half(delta_packed, share, 0)),
            spread(column_sum(delta_uquery)),
            spread(column_sum(delta_uvalues)),
            column_sum(delta_own),
        ]
        vec_grads = jnp.stack(
            bias_grads + known
        )
        vec_grads = vec_grads.reshape(13, 2 * chips, part).transpose(1, 0, 2).reshape(2 * chips, 13 * part)
        vec_grads = jnp.concatenate([vec_grads, column_sum(delta_hidden_in).reshape(2 * chips, -1)], axis=1)
        vec_grads = jnp.pad(vec_grads, ((0, 0), (0, 1024 - vec_grads.shape[1])))
        reduce = lambda values, axis: lax.psum_scatter(values, "seq", scatter_dimension=axis, tiled=True)

        def finish(values, axis):
            return join(half(values, share, axis), swap(half(values, 1 - share, axis)), axis + 1)

        proj_o = finish(reduce(jnp.stack([delta_proj0, delta_proj1, delta_proj2, delta_proj3, delta_proj4, delta_proj5]), 1), 1)
        maps_o = finish(reduce(jnp.stack([delta_map0, delta_map1]), 1), 1)
        expand_o = finish(reduce(delta_expand, 0), 0)
        shrink_o = finish(reduce(delta_shrink, 0), 0)
        vec_o = lax.psum_scatter(vec_grads, AXES, scatter_dimension=0, tiled=True).reshape(-1)
        small = vec_o[: 13 * part].reshape(13, part)
        expand_small = vec_o[13 * part : 13 * part + hidden // (2 * chips)]
    return (
        new_tokens,
        new_memory,
        tokens_grad,
        memory_grad,
        proj_o,
        maps_o,
        expand_o,
        shrink_o,
        small[0:6],
        small[6:9],
        small[9:12],
        expand_small,
        small[12],
    )


def solution(mesh):
    rows, stacked = P(AXES, None), P(None, AXES, None)
    table, line = P(None, AXES), P(AXES)
    custom = mesh.shape["seq"] == 16 and mesh.shape["mem"] == 2
    return jax.shard_map(
        functools.partial(body, custom),
        mesh=mesh,
        in_specs=(rows, rows, P("seq"), rows, rows, stacked, stacked, rows, rows, table, table, table, line, line),
        out_specs=(rows, rows, rows, rows, stacked, stacked, rows, rows, table, table, table, line, line),
        check_vma=False,
    )
```

profile of v0, /device:TPU:0, one launch (start us, length us, event | category | flops | bytes accessed | tf_op | source)
XLA Modules:
  0.0 226.1 jit_solution(10002169817594432187)
XLA Ops:
  1.3 117.1 %gather_and_forward.1 = (bf16[6,4,2,2,48,384]{5,4,3,2,1,0:T(8,128)(2,1)}, bf16[2,4,2,2,48,768]{5,4,3,2,1,0:T(8,128)(2,1)}, bf16[4,2,2,48,3072]{4,3,2,1,0:T(8,128...) custom-call(f32[6,24,768]{2,1,0:T(8,128)} %proj_in.1, ...), custom_call_target="tpu_custom_call" | custom-call | tf_op jit(solution)/shard_map/gather_and_forward/pallas_call | solution.py:689
  118.4 102.2 %backward_and_sums.1 = (f32[6,24,768]{2,1,0:T(8,128)}, f32[2,24,768]{2,1,0:T(8,128)}, f32[24,3072]{1,0:T(8,128)}, f32[96,768]{1,0:T(8,128)}, f32[24,768]{1,0:T(8...) custom-call(f32[24,768]{1,0:T(8,128)} %get-tuple-element.64.table, f32[24,768]{1,0:T(8,128)} %get-tuple-element.65.vectors_in, ...), custom_call_target="tpu_custom_call" | custom-call | tf_op jit(solution)/shard_map/backward_and_sums/pallas_call | solution.py:1138
  220.6 5.3 %deliver.1 = (f32[512,768]{1,0:T(8,128)}, f32[128,768]{1,0:T(8,128)}, f32[512,768]{1,0:T(8,128)}, f32[128,768]{1,0:T(8,128)}, f32[6,24,768]{2,1,0:T(8,128)}, /*i...) custom-call(f32[512,768]{1,0:T(8,128)} %get-tuple-element.62.refs_0_, ...), custom_call_target="tpu_custom_call" | custom-call | tf_op jit(solution)/shard_map/deliver/pallas_call | solution.py:1207
where the time goes:
time: 230 us; the launch traced here: 226 us
  Pallas kernels  225 us (98%)
    pallas_call x1, Pallas kernels, gather_chips(): pl.pallas_call(functools.partial(gather_kernel, far_count), out_shape=[ja...  117 us
    pallas_call x1, Pallas kernels, reduce_chips(): pl.pallas_call(functools.partial(reduce_kernel, far_count), out_shape=[ja...  102 us
    pallas_call x1, Pallas kernels, deliver(): pl.pallas_call(functools.partial(deliver_kernel, len(arrays)), out_shape=...  5.34 us

commit v1 on v0

--- a/solution.py
+++ b/solution.py
@@ -57,22 +57,21 @@
 
 FORWARD = (
     (0, 0), (15, 0), (16, 0), (0, 1), (15, 1), (1, 0), (16, 1), (0, 2), (0, 3), (2, 0), (1, 1), (3, 0), (2, 1),
-    (1, 2), "q", (3, 1), (4, 0), (2, 2), "k", (5, 0), (3, 2), "v", "pf0", (4, 1), (6, 0), "pf1", (5, 1), "pf2", "cx",
-    (7, 0), (4, 2), (6, 1), (4, 3), "yp", (5, 2), (8, 0), "ln0", (7, 1), (9, 0), (6, 2), "ku", (8, 1), (10, 0),
-    (7, 2), "qu", "uf0", (9, 1), (11, 0), "uf1", "uf2", (8, 2), (10, 1), (12, 0), "ux", (8, 3), (9, 2), "att",
-    (9, 3), (11, 1), (13, 0), (10, 2), (12, 1), (14, 0), (10, 3), "w0", "w2", (11, 2), (13, 1), (11, 3), (12, 2),
-    (14, 1), (12, 3), "w1", "w3", (13, 2), (14, 2), (13, 3), (14, 3), (15, 2), (15, 3), (16, 2), (16, 3), "nar",
+    (1, 2), 1, (3, 1), (4, 0), (2, 2), 0, (5, 0), (3, 2), 2, 11, (4, 1), (6, 0), 13, (5, 1), 15, 3,
+    (7, 0), (4, 2), (6, 1), (4, 3), 4, (5, 2), (8, 0), 5, (7, 1), (9, 0), (6, 2), 6, (8, 1), (10, 0),
+    (7, 2), 7, 12, (9, 1), (11, 0), 14, 16, (8, 2), (10, 1), (12, 0), 8, (8, 3), (9, 2), 9,
+    (9, 3), (11, 1), (13, 0), (10, 2), (12, 1), (14, 0), (10, 3), 17, 19, (11, 2), (13, 1), (11, 3), (12, 2),
+    (14, 1), (12, 3), 18, 20, (13, 2), (14, 2), (13, 3), (14, 3), (15, 2), (15, 3), (16, 2), (16, 3), 10,
 )
 BACKWARD = (
-    (0, 0), (1, 0), "dha", "dhb", (2, 0), (3, 0), "de0", (0, 1), (1, 1), "de1", (0, 2), (1, 2), "dm0", (2, 1),
-    (3, 1), "dm1", (2, 2), (3, 2), (4, 0), (5, 0), "mix", (1, 3), (0, 3), "gm1", "ua0", (2, 3), (3, 3), "ua1",
-    (6, 0), (7, 0), (4, 1), (5, 1), "ua2", (1, 4), "pk", (4, 2), (5, 2), "g3", (0, 4), "g45", (6, 1), (7, 1), "gm0",
-    (2, 4), (6, 2), (7, 2), "pa0", (8, 0), (5, 3), (4, 3), (9, 0), "pa1", (3, 4), "pa2", (6, 3), (7, 3), (10, 0),
-    (11, 0), "g0", (8, 1), (9, 1), (5, 4), "g12", (8, 2), (9, 2), (16, 0), "tok0", (4, 4), (16, 1), "out0", (10, 1),
-    (11, 1), "out1", "fin", (6, 4), (10, 2), (11, 2), (12, 0), (9, 3), (8, 3), (13, 0), (7, 4), (16, 2), (11, 3),
-    (10, 3), (9, 4), (14, 0), (12, 1), (13, 1), (12, 2), (8, 4), (15, 0), (16, 3), (13, 2), (14, 1), (12, 3),
-    (11, 4), (14, 2), (15, 1), (10, 4), (13, 3), (15, 2), (15, 3), (14, 3), (16, 4), (12, 4), (13, 4), (15, 4),
-    (14, 4),
+    (0, 0), (1, 0), (2, 0), (3, 0), 0, 0, 0, (2, 1), (3, 1), 0, (4, 0), (5, 0), (2, 2), (3, 2),
+    0, 0, (2, 3), (3, 3), (6, 0), (7, 0), 0, (4, 1), (5, 1), 0, (0, 1), (4, 2), (5, 2), 0, 0,
+    (6, 1), (7, 1), 0, 0, (6, 2), (7, 2), 0, 0, (9, 0), (4, 3), (5, 3), 0, (0, 2), (8, 0), 0,
+    (1, 1), (6, 3), (7, 3), 0, (9, 1), 0, (8, 1), (2, 4), (9, 2), 0, (0, 3), (8, 2), (10, 0), (11, 0),
+    (1, 2), (3, 4), 0, (9, 3), (16, 0), 0, (8, 3), (4, 4), (16, 1), 0, (10, 1), (11, 1), 0,
+    (5, 4), 0, (10, 2), (1, 3), (11, 2), (12, 0), (13, 0), (16, 2), (6, 4), (11, 3), (10, 3), (7, 4), (12, 1),
+    (13, 1), (12, 2), (9, 4), (13, 2), (14, 0), (15, 0), (16, 3), (8, 4), (12, 3), (13, 3), (15, 1), (11, 4),
+    (14, 1), (15, 2), (14, 2), (10, 4), (16, 4), (14, 3), (15, 3), (12, 4), (13, 4), (14, 4), (15, 4),
 )
 
 
@@ -269,8 +268,26 @@
         self.held[k] = self._take(k - 1)
         self._go(k)
 
-    def result(self):
-        return self._take(3)
+    def scatter(self, far_in, cuts):
+        self.held[3] = self._take(2)
+        self.flying = []
+        for k, device in enumerate(self.to["far"]):
+            for n, (rows, columns) in enumerate(cuts(self.to["far_index"][k])):
+                copy = pltpu.make_async_remote_copy(
+                    self.held.at[3, rows, columns], far_in.at[k, rows], self.sems[0].at[3 + 2 * k + n], self.sems[1].at[3 + 2 * k + n],
+                    device_id=device, device_id_type=MESH,
+                )
+                copy.start()
+                self.flying.append(copy)
+
+    def gathered(self, far_in, own_cuts, target):
+        for copy in self.flying:
+            copy.wait()
+        for rows, columns in own_cuts:
+            value = self.held[3, rows, columns]
+            for k in range(len(self.to["far"])):
+                value = value + far_in[k, rows]
+            target[rows] = value
 
 
 def attention_forward(pairs, queries, keys, values, valid, probs, mixed, first_lane, turned):
@@ -592,26 +609,26 @@
         for source, target in ((d_sum2, d_sum2_o), (d_branch, d_branch_o), (new_tokens, new_tokens_o), (grad_table, grad_table_o)):
             store(source, target)
 
-    work = {
-        "k": make_k,
-        "q": make_q,
-        "v": lambda: project(2, inputs, vp, 1),
-        "cx": lambda: cross(2, mixed_p.at[:, span(core)], mixed_p.at[:, span(core)]),
-        "yp": make_packed,
-        "ln0": make_memory,
-        "ku": make_unpack,
-        "qu": lambda: project(3, inputs, qu, 3),
-        "ux": lambda: cross(3, mixed_u.at[:, span(core)], mixed_u.at[:, span(core)]),
-        "att": make_middle,
-        "nar": make_tokens,
-    }
+    work = [
+        make_k,
+        make_q,
+        lambda: project(2, inputs, vp, 1),
+        lambda: cross(2, mixed_p.at[:, span(core)], mixed_p.at[:, span(core)]),
+        make_packed,
+        make_memory,
+        make_unpack,
+        lambda: project(3, inputs, qu, 3),
+        lambda: cross(3, mixed_u.at[:, span(core)], mixed_u.at[:, span(core)]),
+        make_middle,
+        make_tokens,
+    ]
     for n in range(3):
-        work["pf" + str(n)] = functools.partial(attention_forward, (n, n + 1), qp, kp, vp, length, probs_p, mixed_p, core * wide, False)
-        work["uf" + str(n)] = functools.partial(attention_forward, (n, n + 1), qu, ku, vu, None, probs_u, mixed_u, core * wide, True)
+        work.append(functools.partial(attention_forward, (n, n + 1), qp, kp, vp, length, probs_p, mixed_p, core * wide, False))
+        work.append(functools.partial(attention_forward, (n, n + 1), qu, ku, vu, None, probs_u, mixed_u, core * wide, True))
     for n in range(4):
-        work["w" + str(n)] = functools.partial(widen, n)
+        work.append(functools.partial(widen, n))
     for item in FORWARD:
-        if isinstance(item, str):
+        if isinstance(item, int):
             work[item]()
             continue
         index, stage = item
@@ -781,6 +798,59 @@
             self._copy(ref, ref, k, self.to["core"]).wait_send()
 
 
+class ReduceNear(Reduce):
+    def __init__(self, where, to, first, at, far_in, half_in, last_in, sems):
+        super().__init__(where, to, first, at, half_in, last_in, far_in, sems)
+
+    def _line(self, other):
+        far, row, column = self.where
+        if self.second == "row":
+            return self.at(far, 1 - row if other else row, slice(None))
+        return self.at(far, slice(None), 1 - column if other else column)
+
+    def _block(self, other):
+        far, row, column = self.where
+        if other:
+            row, column = (1 - row, column) if self.first == "row" else (row, 1 - column)
+        return self.at(far, row, column)
+
+    def step(self, stage):
+        far = self.where[0]
+        count = len(self.to["far"])
+        if stage == 0:
+            for k, device in enumerate(self.to["far"]):
+                self._go(self.at(self.to["far_index"][k], slice(None), slice(None)), self.far_in.at[k], k, device)
+        if stage == 1:
+            for k in range(count):
+                self._arrived(self.far_in.at[k], k)
+            plane = self.at(far, slice(None), slice(None))
+            for r in range(2):
+                for c in range(2):
+                    value = plane[r, c].astype(F32)
+                    for k in range(count):
+                        value = value + self.far_in[k, r, c].astype(F32)
+                    plane[r, c] = value.astype(LOW)
+            self._go(self._line(True), self.half_in, count, self.to[self.second])
+        if stage == 2:
+            self._arrived(self.half_in, count)
+            self._add(self._line(False), self.half_in)
+            self._go(self._block(True), self.quarter_in, count + 1, self.to[self.first])
+        if stage == 3:
+            self._arrived(self.quarter_in, count + 1)
+
+    def result(self):
+        return self._block(False)[...].astype(F32) + self.quarter_in[...].astype(F32)
+
+    def finish(self):
+        refs = [self.far_in.at[k] for k in range(len(self.to["far"]))] + [self.half_in, self.quarter_in]
+        for k, ref in enumerate(refs):
+            self._copy(ref, ref, k, self.to["core"]).wait_send()
+
+
+def window(start, width):
+    return lax.min(lax.div(start, 128), width // 128 - 2)
+
+
 def attention_backward(pairs, queries, keys, values, probs, mixed, d_query, d_key, d_value, turned):
     scale = HEAD ** (-0.5)
     for pair in range(*pairs):
@@ -806,8 +876,8 @@
 
 def reduce_kernel(far_count, table, vectors_in, hidden_h, d_branch_x_h, d_branch_h, slope_h, expand_h, shrink_h, middle_h, d_sum2_h, middle_sum_h,
                   mixed_u_h, mixed_p_h, inputs_h, memory_h, qu_h, ku_h, vu_h, qp_h, kp_h, vp_h, probs_u_h, probs_p_h, packed_h, d_sum0_h, proj_h, maps_h,
-                  proj_o, maps_o, expand_o, shrink_o, vec_o, tokens_o, memory_o,
-                  half_in, quarter_in, far_in, vec_sum, vec_in, sums,
+                  proj_o, maps_o, expand_o, shrink_o, vec_o, tokens_out, memory_out,
+                  tokens_o, memory_o, near_in, near_half, near_last, vec_far, half_in, quarter_in, far_in, vec_sum, vec_in, sums,
                   grads, expand_grads, shrink_grads, d_hidden_x, d_unpacked, d_sum1, partial, partial_in, wide_out, wide_in, rows_out, rows_in,
                   send, recv, last_send, last_recv, last_local, in_sems, cross_send, cross_recv, vec_send, vec_recv):
     seq, core = lax.axis_index("seq"), lax.axis_index("mem")
@@ -844,7 +914,10 @@
     def add(at, end):
         k = len(units)
         first = "column" if k % 2 == 0 else "row"
-        units.append(Reduce(where, to, first, at, half_in.at[k], quarter_in.at[k], far_in.at[k], (send.at[k], recv.at[k])))
+        if k < 2:
+            units.append(ReduceNear(where, to, first, at, near_in.at[k], near_half.at[k], near_last.at[k], (send.at[k], recv.at[k])))
+        else:
+            units.append(Reduce(where, to, first, at, half_in.at[k - 2], quarter_in.at[k - 2], far_in.at[k - 2], (send.at[k], recv.at[k])))
         ends.append(end)
 
     def add_expand(k):
@@ -867,7 +940,17 @@
     for make, p in ((add_map, 1), (add_proj, 3), (add_proj, 4), (add_proj, 5), (add_map, 0), (add_proj, 0), (add_proj, 1), (add_proj, 2)):
         make(p)
 
-    bias_sums = Vectors(to, vec_sum, vec_in, vec_send, vec_recv, ("core", "column", "row", "far"))
+    bias_sums = Vectors(to, vec_sum, vec_in, vec_send, vec_recv, ("core", "column", "row"))
+    chips = 4 * far_count
+    large = expand_o.shape[1] // (2 * chips)
+
+    def cuts(far):
+        device = 2 * (far * 4 + lax.rem(seq, 4)) + core
+        return tuple(
+            (rows_of, pl.ds(pl.multiple_of(128 * window(start, width), 128), 256))
+            for rows_of, start in ((pl.ds(0, 16), part * device), (pl.ds(16, 8), lax.rem(large * device, width)))
+        )
+
 
     def last(k, source, target):
         return pltpu.make_async_remote_copy(source, target, last_send.at[k], last_recv.at[k], device_id=to["core"], device_id_type=MESH)
@@ -909,25 +992,25 @@
 
     place_in_plan = [0]
 
-    def turn(name):
+    def turn():
         while place_in_plan[0] < len(BACKWARD):
             item = BACKWARD[place_in_plan[0]]
             place_in_plan[0] += 1
-            if isinstance(item, str):
-                if item != name:
-                    raise ValueError(item)
+            if isinstance(item, int):
                 return
             index, stage = item
             if index == 16:
                 if stage == 0:
                     bias_sums.start()
-                elif stage < 4:
+                elif stage < 3:
                     bias_sums.step(stage)
+                elif stage == 3:
+                    bias_sums.scatter(vec_far, cuts)
                 else:
-                    vec_o[...] = bias_sums.result()
+                    bias_sums.gathered(vec_far, cuts(where[0]), vec_o)
                 continue
             units[index].step(stage)
-            if stage == 4:
+            if stage == (3 if index < 2 else 4):
                 sums[index] = units[index].result()
                 close(index, True)
 
@@ -974,7 +1057,7 @@
         sent = []
         for k in range(4):
             if k % 2 == 0:
-                turn("dha" if k == 0 else "dhb")
+                turn()
             which = 1 - core if k < 2 else core
             piece = which * 2 + k % 2
             columns = pl.ds(pl.multiple_of(piece * quarter, 128), quarter)
@@ -982,7 +1065,7 @@
             value = against(d_branch[...], shrink_w[pl.ds(piece * (quarter // tall), quarter // tall)].reshape(quarter, width))
             value = (value * slope[:, columns].astype(F32)).astype(LOW)
             slope[:, columns] = value
-            vec_sum[0, pl.ds(13 + piece, 1), :] = total_rows(value.astype(F32))
+            vec_sum[0, pl.ds(16 + piece, 1), :] = total_rows(value.astype(F32))
             if k < 2:
                 sent.append(cross(3 + k, slope.at[:, columns], d_hidden_x.at[own, here]))
             else:
@@ -999,9 +1082,9 @@
             for j in range(2):
                 expand_grads[2 * k + j] = value[:, j * wide : (j + 1) * wide].reshape(expand_grads.shape[1:])
 
-        turn("de0")
+        turn()
         one(0)
-        turn("de1")
+        turn()
         one(1)
         need("expand", "d_sum2", "middle_sum")
         vec_sum[0, 5:6] = jnp.zeros((1, width), F32)
@@ -1021,9 +1104,9 @@
             vec_sum[0, 5:6] += total_rows(low.astype(F32))
             return carry
 
-        turn("dm0")
+        turn()
         lax.fori_loop(0, own_rows // 512, two, 0)
-        turn("dm1")
+        turn()
         lax.fori_loop(own_rows // 512, own_rows // 256, two, 0)
         return cross(5, d_unpacked.at[own], d_unpacked.at[own])
 
@@ -1053,28 +1136,28 @@
         def from_map_u(piece):
             d_mixed[piece] = against(d_unpacked[piece], map_u[...]).astype(LOW)
 
-        turn("mix")
+        turn()
         from_map_u(slice(None))
         need("mixed_u")
-        turn("gm1")
+        turn()
         weight_grad((7,), mixed_u, d_unpacked[:, span(core)])
         need("qu", "ku", "vu", "probs_u")
         for n in range(3):
-            turn("ua" + str(n))
+            turn()
             attention_backward((n, n + 1), qu, ku, vu, probs, d_mixed, d_query, d_key, d_value, True)
         below((("probs_p", probs_p_h, probs),))
         need("inputs", "packed", "weights", "d_sum0")
-        turn("pk")
+        turn()
         partial[...] = against(d_key[...], weights[4]) + against(d_value[...], weights[5])
         packing = cross(0, partial, partial_in)
-        turn("g3")
+        turn()
         weight_grad((3,), inputs, d_query[...])
-        turn("g45")
+        turn()
         weight_grad((4, 5), packed, d_key[...], d_value[...])
         put_bias(3, d_query[...])
         put_bias(4, d_value[...])
 
-        turn("gm0")
+        turn()
         packing.wait()
         d_packed[...] = (d_sum0[...] + (partial[...] + partial_in[...])).astype(LOW)
         need("map_p", "mixed_p")
@@ -1084,32 +1167,40 @@
         vec_sum[0, 2:3, :] = total_rows(d_packed[pl.ds(pl.multiple_of(core * mem_rows, 128), mem_rows)].astype(F32))
         need("qp", "kp", "vp", "probs_p")
         for n in range(3):
-            turn("pa" + str(n))
+            turn()
             attention_backward((n, n + 1), qp, kp, vp, probs, d_mixed_p, d_key, d_token_key, d_token_value, False)
         need("memory")
-        turn("g0")
+        turn()
         weight_grad((0,), memory, d_key[...])
-        turn("g12")
+        turn()
         weight_grad((1, 2), inputs, d_token_key[...], d_token_value[...])
         put_bias(0, d_key[...])
         put_bias(1, d_token_value[...])
-        turn("tok0")
+        turn()
         own_mem = pl.ds(pl.multiple_of(core * mem_rows, 128), mem_rows)
         other_mem = pl.ds(pl.multiple_of((1 - core) * mem_rows, 128), mem_rows)
         rows_out[...] = against(d_key[...], weights[0])
         memory_terms = cross(2, rows_out.at[other_mem], rows_in)
         wide_out[...] = against(d_query[other], weights[3]) + against(d_token_key[other], weights[1]) + against(d_token_value[other], weights[2])
         token_terms = cross(1, wide_out, wide_in)
-        turn("out0")
+        turn()
         tokens_o[...] = d_sum1[...] + against(d_query[own], weights[3])
-        turn("out1")
+        turn()
         tokens_o[...] = tokens_o[...] + against(d_token_key[own], weights[1]) + against(d_token_value[own], weights[2])
-        turn("fin")
+        turn()
         memory_terms.wait()
         memory_o[...] = d_sum0[own_mem] + rows_out[own_mem] + rows_in[...]
         token_terms.wait()
         tokens_o[...] = tokens_o[...] + wide_in[...]
-        turn(None)
+        copies = [
+            pltpu.make_async_copy(source, target, in_sems.at[28 + k])
+            for k, (source, target) in enumerate(((tokens_o, tokens_out), (memory_o, memory_out)))
+        ]
+        for copy in copies:
+            copy.start()
+        turn()
+        for copy in copies:
+            copy.wait()
         for k in range(len(units)):
             close(k, False)
         for unit in units:
@@ -1134,18 +1225,24 @@
     grid = (far_count, 2, 2)
     any_space = pl.BlockSpec(memory_space=pl.ANY)
     vmem = pl.BlockSpec(memory_space=pltpu.VMEM)
-    shapes = ((6, part, width), (2, part, width), (part, hidden), (hidden // (8 * far_count), width), vectors.shape, d_sum2.shape, (all_rows // 2, width))
+    shapes = ((6, part, width), (2, part, width), (part, hidden), (hidden // (8 * far_count), width), (24, 256), d_sum2.shape, (all_rows // 2, width))
     return pl.pallas_call(
         functools.partial(reduce_kernel, far_count),
         out_shape=[jax.ShapeDtypeStruct(shape, F32) for shape in shapes],
         in_specs=[vmem] + [any_space] * (1 + len(arrays)),
-        out_specs=[vmem] * 7,
+        out_specs=[any_space] * 4 + [vmem] + [any_space] * 2,
         scratch_shapes=[
-            pltpu.VMEM((16, 2, far_count, rows, wide), LOW),
-            pltpu.VMEM((16, far_count, rows, wide), LOW),
-            pltpu.VMEM((16, far_count - 1, rows, wide), LOW),
+            pltpu.VMEM(shapes[5], F32),
+            pltpu.VMEM(shapes[6], F32),
+            pltpu.VMEM((2, far_count - 1, 2, 2, rows, wide), LOW),
+            pltpu.VMEM((2, 2, rows, wide), LOW),
+            pltpu.VMEM((2, rows, wide), LOW),
+            pltpu.VMEM((far_count - 1, 24, 256), F32),
+            pltpu.VMEM((14, 2, far_count, rows, wide), LOW),
+            pltpu.VMEM((14, far_count, rows, wide), LOW),
+            pltpu.VMEM((14, far_count - 1, rows, wide), LOW),
             pltpu.VMEM((4,) + vectors.shape, F32),
-            pltpu.VMEM((2 + far_count,) + vectors.shape, F32),
+            pltpu.VMEM((3,) + vectors.shape, F32),
             pltpu.VMEM((16, rows, wide), F32),
             pltpu.VMEM((8,) + grid + (rows, wide), LOW),
             pltpu.VMEM((4,) + grid + (rows, wide), LOW),
@@ -1167,8 +1264,8 @@
             pltpu.SemaphoreType.DMA((34,)),
             pltpu.SemaphoreType.DMA((6,)),
             pltpu.SemaphoreType.DMA((6,)),
-            pltpu.SemaphoreType.DMA((2 + far_count,)),
-            pltpu.SemaphoreType.DMA((2 + far_count,)),
+            pltpu.SemaphoreType.DMA((2 * far_count + 1,)),
+            pltpu.SemaphoreType.DMA((2 * far_count + 1,)),
         ],
         compiler_params=pltpu.CompilerParams(
             collective_id=1, has_side_effects=True, vmem_limit_bytes=62 << 20
@@ -1185,15 +1282,19 @@
     for copy in loads:
         copy.start()
     device = 2 * lax.axis_index("seq") + lax.axis_index("mem")
-    width = table.shape[1]
     small, large = vectors[0].shape[1], vectors[3].shape[1]
-    turned = pltpu.roll(table[0:16], lax.rem(width - small * device, width), 1)[:, 0:small]
+    width = targets[0].shape[1]
+
+    def turn(values, start):
+        return pltpu.roll(values, lax.rem(256 - (start - 128 * window(start, width)), 256), 1)
+
+    turned = turn(table[0:16], small * device)[:, 0:small]
     vectors[0][...] = turned[0:6]
     vectors[1][...] = turned[6:9]
     vectors[2][...] = turned[9:12]
     vectors[4][...] = turned[12:13]
     row, column = lax.div(large * device, width), lax.rem(large * device, width)
-    vectors[3][...] = pltpu.roll(table[pl.ds(13 + row, 1)], lax.rem(width - column, width), 1)[:, 0:large]
+    vectors[3][...] = turn(table[pl.ds(16 + row, 1)], column)[:, 0:large]
     for load, copy in zip(loads, stores):
         load.wait()
         copy.start()

time: 230 us -> 220 us (0.957)
  Pallas kernels: 225 us -> 215 us
    pallas_call x1, Pallas kernels: 102 us -> 92.7 us  [reduce_chips(): pl.pallas_call(functools.partial(reduce_kernel, far_count), out_shape=[ja...]
where the time goes in v1:
time: 220 us; the launch traced here: 216 us
  Pallas kernels  215 us (98%)
    pallas_call x1, Pallas kernels, gather_chips(): pl.pallas_call(functools.partial(gather_kernel, far_count), out_shape=[ja...  117 us
    pallas_call x1, Pallas kernels, reduce_chips(): pl.pallas_call(functools.partial(reduce_kernel, far_count), out_shape=[ja...  92.7 us
    pallas_call x1, Pallas kernels, deliver(): pl.pallas_call(functools.partial(deliver_kernel, len(arrays)), out_shape=...  5.19 us

profile of v1, /device:TPU:0, one launch (start us, length us, event | category | flops | bytes accessed | tf_op | source)
XLA Modules:
  0.0 216.4 jit_solution(16761967418469172173)
XLA Ops:
  1.3 117.1 %gather_and_forward.1 = (bf16[6,4,2,2,48,384]{5,4,3,2,1,0:T(8,128)(2,1)}, bf16[2,4,2,2,48,768]{5,4,3,2,1,0:T(8,128)(2,1)}, bf16[4,2,2,48,3072]{4,3,2,1,0:T(8,128...) custom-call(f32[6,24,768]{2,1,0:T(8,128)} %proj_in.1, ...), custom_call_target="tpu_custom_call" | custom-call | tf_op jit(solution)/shard_map/gather_and_forward/pallas_call | solution.py:706
  118.4 92.7 %backward_and_sums.1 = (f32[6,24,768]{2,1,0:T(8,128)}, f32[2,24,768]{2,1,0:T(8,128)}, f32[24,3072]{1,0:T(8,128)}, f32[96,768]{1,0:T(8,128)}, f32[24,256]{1,0:T(8...) custom-call(f32[24,768]{1,0:T(8,128)} %get-tuple-element.64.table, f32[24,768]{1,0:T(8,128)} %get-tuple-element.65.vectors_in, ...), custom_call_target="tpu_custom_call" | custom-call | tf_op jit(solution)/shard_map/backward_and_sums/pallas_call | solution.py:1229
  211.0 5.2 %deliver.1 = (f32[512,768]{1,0:T(8,128)}, f32[128,768]{1,0:T(8,128)}, f32[512,768]{1,0:T(8,128)}, f32[128,768]{1,0:T(8,128)}, f32[6,24,768]{2,1,0:T(8,128)}, /*i...) custom-call(f32[512,768]{1,0:T(8,128)} %get-tuple-element.62.refs_0_, ...), custom_call_target="tpu_custom_call" | custom-call | tf_op jit(solution)/shard_map/deliver/pallas_call | solution.py:1308
